TPU v7x, 256 devices: a whole 4x4x8 slice. The times are simulated.
256 devices in a mesh: term: 32 (over z_lo, y, core), wave: 8 (over x, z_hi).
Axes of the slice: x: 4, y: 4, z: 8 (z_hi: 2, z_lo: 4; z = z_hi * 4 + z_lo), core: 2. Of those that a mesh axis runs over, the one named last changes fastest.
Arguments:
- spectral_state: bfloat16 [32, 512, 1280], P('wave', 'term'), may hold values from -6 to 6
- inverse: bfloat16 [32, 32, 2, 640, 640], P('term', 'wave'), may hold values from -0.15625 to 0.15625
- term_weights: float32 [32, 2], P('term'), may hold values from -2.5 to 2.5
- legendre: bfloat16 [32, 640, 1280], P('wave'), may hold values from -0.25 to 0.25
- slot_column: int32 [32], replicated, may hold values from 0 to 31, each once
Outputs:
- fourier: float32 [32, 2, 512, 1280], P(None, None, 'term', 'wave')
Inputs may be any that keep to these rules, and one draw needn't show every extreme that they name: `slot_column`: each column appears in exactly one slot.
All inputs are finite; a program needn't handle non-finite values.
Results may differ from a plain program's by a relative error of at most 0.0003.
Values may be sent and summed in bfloat16 or wider, within the bound.
A program may use at most 128 MiB of HBM per device.

v0:
```python
import jax
import jax.numpy as jnp
from jax import lax
from jax.sharding import Mesh
from jax.sharding import PartitionSpec as P

TERM = ("term_0", "term_1", "term_2")


def cut_along(array, dim, peers):
    before, after = (array.shape[:dim], array.shape[dim + 1 :])
    return jnp.moveaxis(array.reshape(*before, peers, -1, *after), dim, 0)


def summed_rows(array, chips, core, dim):
    sizes = (lax.axis_size(chips), lax.axis_size(core))
    pieces = cut_along(array, dim, sizes[0] * sizes[1])
    inside = pieces.shape[1:]
    pieces = pieces.reshape(*sizes, *inside).swapaxes(0, 1).reshape(-1, *inside)
    pieces = lax.psum_scatter(pieces, core, scatter_dimension=0, tiled=True)
    return lax.psum_scatter(pieces, chips, scatter_dimension=0, tiled=True)[0]


def exact_product(values, table):
    return jnp.einsum(
        "spcn,snl->spcl", values, table.astype(jnp.float32), precision=lax.Precision.HIGHEST
    )


def shards(spectral_state, inverse, term_weights, legendre, slot_column):
    whole = lax.all_gather(spectral_state, TERM, axis=1, tiled=True)
    middle = whole.shape[2] // 2
    column_count = whole.shape[1]
    stacked = jnp.concatenate([whole[:, :, :middle], whole[:, :, middle:]], axis=1)
    real_image = jnp.einsum(
        "srn,ksno->ksro", stacked, inverse[:, :, 0], preferred_element_type=jnp.float32
    )
    imag_image = jnp.einsum(
        "srn,ksno->ksro", stacked, inverse[:, :, 1], preferred_element_type=jnp.float32
    )
    solved_re = real_image[:, :, :column_count] - imag_image[:, :, column_count:]
    solved_im = imag_image[:, :, :column_count] + real_image[:, :, column_count:]
    weight_re = term_weights[:, 0][:, None, None, None]
    weight_im = term_weights[:, 1][:, None, None, None]
    total_re = jnp.sum(weight_re * solved_re - weight_im * solved_im, axis=0)
    total_im = jnp.sum(weight_re * solved_im + weight_im * solved_re, axis=0)
    partial_value = jnp.stack([total_re, total_im], axis=1)
    mine = summed_rows(partial_value, ("term_0", "term_1"), "term_2", 2)
    grid = exact_product(mine, legendre)
    bands = lax.all_to_all(grid, "wave", split_axis=3, concat_axis=0, tiled=True)
    slot_count = slot_column.shape[0]
    selector = (slot_column[:, None] == jnp.arange(slot_count, dtype=jnp.int32)[None, :]).astype(
        jnp.float32
    )
    return jnp.einsum("spcl,sq->qpcl", bands, selector, precision=lax.Precision.HIGHEST)


def solution(mesh):
    finer = Mesh(
        mesh.devices.reshape(4, 4, 2, mesh.shape["wave"]), ("term_0", "term_1", "term_2", "wave")
    )
    placed = (
        P("wave", TERM, None),
        P(TERM, "wave", None, None, None),
        P(TERM, None),
        P("wave", None, None),
        P(),
    )
    return jax.shard_map(
        shards, mesh=finer, in_specs=placed, out_specs=P(None, None, TERM, "wave"), check_vma=False
    )
```

profile of v0, /device:TPU:32, one launch (start us, length us, event | category | flops | bytes accessed | tf_op | source)
XLA Modules:
  0.0 301.8 jit_solution(1209462435278588881)
XLA Ops:
  6.5 0.0 all-gather.2.cloned.1.call-start
  6.5 0.7 all-gather.2.cloned.1.call-update
  7.3 0.0 reduce-scatter.3.cloned.1.call-start
  7.3 1.3 fusion.14
  8.6 66.9 %all-gather.2.cloned.1.call-done = bf16[4,512,1280]{2,1,0:T(8,128)(2,1)} async-done(((bf16[4,16,1280]{2,1,0:T(8,128)(2,1)}), bf16[4,512,1280]{2,1,0:T(8,128)(2,1)}) %all-gather.2.cloned.1.call-update) | async-done | bytes 5242896 | tf_op jit(solution)/shard_map/all_gather | solution.py:31
  75.5 3.0 fusion.13
  78.5 6.7 %convolution_bitcast_fusion.1 = f32[1,4,1024,640]{3,2,1,0:T(8,128)S(1)} fusion(bf16[4,512,640]{2,1,0:T(8,128)(2,1)S(1)} %get-tuple-element.8, bf16[4,512,640]{2,1,0:T(8,128)(2,1)S(1)} %get-tuple-element.7, bf16[1,4,2,640,640]{4,3,2,1,0:T(8,128)(2,1)} %param.6), kind=kOutput, calls=%fused_computation.9 | convolution fusion | flops 3365928960 | bytes 19005440 | tf_op jit(solution)/shard_map/srn,ksno->ksro/dot_general | solution.py:35
  85.2 10.2 %convolution_bitcast_fusion = f32[1,4,1024,640]{3,2,1,0:T(8,128)} fusion(bf16[4,512,640]{2,1,0:T(8,128)(2,1)S(1)} %get-tuple-element.8, bf16[4,512,640]{2,1,0:T(8,128)(2,1)S(1)} %get-tuple-element.7, bf16[1,4,2,640,640]{4,3,2,1,0:T(8,128)(2,1)} %param.6), kind=kOutput, calls=%fused_computation.8 | convolution fusion | flops 3365928960 | bytes 19005440 | tf_op jit(solution)/shard_map/srn,ksno->ksro/dot_general | solution.py:38
  95.4 8.3 %multiply_subtract_fusion = (f32[1,4,512,640]{3,2,1,0:T(8,128)}, f32[1,4,512,640]{3,2,1,0:T(8,128)}) fusion(f32[]{:T(128)} %bitcast.11, f32[]{:T(128)} %bitcast.2, f32[1,4,1024,640]{3,2,1,0:T(8,128)} %convolution_bitcast_fusion, f32[1,4,1024,640]{3,2,1,0:T(8,128)S(1)} %convolution_bitcast_fusion.1), kind=kLoop, calls=%fused_computation.7 | loop fusion | flops 10485760 | bytes 31457288 | tf_op jit(solution)/shard_map/sub | solution.py:45
  103.7 5.2 %pad_maximum_fusion = f32[4,2,32,16,640]{4,3,2,0,1:T(8,128)S(1)} fusion(f32[4,1,32,16,640]{4,3,2,0,1:T(8,128)} %bitcast.55, f32[4,1,32,16,640]{4,3,2,0,1:T(8,128)} %bitcast.54), kind=kLoop, calls=%fused_computation | loop fusion | flops 2621440 | bytes 20971520 | tf_op jit(solution)/shard_map/stack | solution.py:47
  108.9 5.6 %copy.13 = f32[16,2,4,2,16,640]{5,4,3,2,0,1:T(8,128)} copy(f32[16,2,4,2,16,640]{5,4,1,0,2,3:T(8,128)S(1)} %bitcast.53) | data formatting | bytes 20971520 | tf_op jit(solution)/shard_map/reshape | solution.py:19
  114.5 0.0 reduce-scatter.3.cloned.1.call-update
  114.5 0.2 reduce-scatter.5.cloned.1.call-start
  114.8 22.7 %reduce-scatter.3.cloned.1.call-done = f32[16,4,2,16,640]{4,3,2,1,0:T(8,128)} async-done(((f32[32,4,2,16,640]{4,3,2,1,0:T(8,128)}), f32[16,4,2,16,640]{4,3,2,1,0:T(8,128)}) %reduce-scatter.3.cloned.1.call-update) | async-done | bytes 5242896 | tf_op jit(solution)/shard_map/reduce_scatter | solution.py:20
  137.5 0.0 reduce-scatter.5.cloned.1.call-update
  137.5 94.4 %reduce-scatter.5.cloned.1.call-done = f32[1,4,2,16,640]{4,3,2,1,0:T(8,128)} async-done(((f32[16,4,2,16,640]{4,3,2,1,0:T(8,128)}), f32[1,4,2,16,640]{4,3,2,1,0:T(8,128)}) %reduce-scatter.5.cloned.1.call-update) | async-done | bytes 327696 | tf_op jit(solution)/shard_map/reduce_scatter | solution.py:21
  231.9 6.0 %fusion = f32[4,2,16,1280]{3,2,1,0:T(8,128)S(1)} fusion(bf16[4,640,1280]{2,1,0:T(8,128)(2,1)} %param.8, f32[1,4,2,16,640]{4,3,2,1,0:T(8,128)} %reduce-scatter.5.cloned.1.call-done), kind=kOutput, calls=%fused_computation.1 | convolution fusion | flops 1258291200 | bytes 7536640 | tf_op jit(solution)/shard_map/spcn,snl->spcl/dot_general | solution.py:25
  237.9 4.9 %copy.14 = f32[4,2,16,1280]{2,1,0,3:T(2,128)} copy(f32[4,2,16,1280]{3,2,1,0:T(8,128)S(1)} %fusion) | data formatting | bytes 1310720 | tf_op jit(solution)/shard_map/spcn,snl->spcl/dot_general | solution.py:25
  242.8 8.8 %reshape.38 = f32[8,1,20480]{2,1,0:T(1,128)S(1)} reshape(f32[1280,4,2,16]{3,2,1,0:T(2,128)} %bitcast.56) | data formatting | bytes 1310720
  251.6 22.9 %all_to_all.18 = f32[8,1,20480]{2,1,0:T(1,128)S(1)} all-to-all(f32[8,1,20480]{2,1,0:T(1,128)S(1)} %reshape.38), channel_id=1, replica_groups=mesh['term_0'=4,'term_1'=4,'term_2'=2,'wave'=8] {'wave'}, dimensions={0} | all-to-all | bytes 1310720 | tf_op jit(solution)/shard_map/all_to_all | solution.py:50
  274.5 0.5 broadcast.3
  275.0 2.2 reduce
  277.2 9.3 %reshape.39 = f32[1280,4,2,16]{3,2,1,0:T(2,128)} reshape(f32[8,20480]{1,0:T(8,128)S(1)} %reduce) | data formatting | bytes 1310720
  286.6 0.0 copy-start
  286.6 6.1 %copy.15 = f32[4,2,16,8,160]{4,0,3,2,1:T(4,128)S(1)} copy(f32[4,2,16,8,160]{2,1,0,4,3:T(2,128)} %bitcast.57) | data formatting | bytes 1310720 | tf_op jit(solution)/shard_map/all_to_all | solution.py:50
  292.7 0.4 all_to_all.16
  293.0 0.0 copy-done
  293.1 0.6 fusion.8
  293.7 1.6 copy.16
Async XLA Ops:
  6.5 68.9 %all-gather.2.cloned.1.call-start = ((), (), s32[]{:S(2)}) async-start(), calls=%async_computation.3 | async-start | bytes 5406720 | tf_op jit(solution)/shard_map/all_gather | solution.py:31
  7.3 130.2 %reduce-scatter.3.cloned.1.call-start = ((), (), s32[]{:S(2)}) async-start(), calls=%async_computation.4 | async-start | bytes 15728640 | tf_op jit(solution)/shard_map/reduce_scatter | solution.py:20
  114.5 117.4 %reduce-scatter.5.cloned.1.call-start = ((), (), s32[]{:S(2)}) async-start(), calls=%async_computation.5 | async-start | bytes 5570560 | tf_op jit(solution)/shard_map/reduce_scatter | solution.py:21
  286.6 6.5 %copy-start = (s32[32]{0:T(128)S(1)}, s32[32]{0:T(128)}, u32[]{:S(2)}) copy-start(s32[32]{0:T(128)} %param.9) | copy-start | bytes 388
Sparse Core Ops, SparseCore 0:
  9.1 66.2 all-gather.1
  114.7 22.7 reduce-scatter.2
  140.1 91.8 reduce-scatter.4
where the time goes:
time: 306 us; the launch traced here: 302 us
  waiting for transfers between devices  185 us (60%)
  local copies, waits for them, and re-layouts  41.4 us (14%)
  matrix products  23.5 us (8%)
  blocking collectives  22.9 us (7%)
  other arithmetic  15.7 us (5%)
  between operations  13.2 us (4%)
    reduce_scatter x1, waiting for transfers between devices, summed_rows(): return lax.psum_scatter(pieces, chips, scatter_dimension=0, tiled=True)[0]  94.4 us
    all_gather x1, waiting for transfers between devices, shards(): whole = lax.all_gather(spectral_state, TERM, axis=1, tiled=True)  66.9 us
    all_to_all x1, blocking collectives, shards(): lax.all_to_all(grid, 'wave', split_axis=3, concat_axis=0, tiled=True)  22.9 us
    reduce_scatter x1, waiting for transfers between devices, summed_rows(): pieces = lax.psum_scatter(pieces, core, scatter_dimension=0, tiled=True)  22.7 us
    unnamed x4, local copies, waits for them, and re-layouts  18.1 us
    dot_general x1, matrix products, shards(): jnp.einsum('srn,ksno->ksro', stacked, inverse[:, :, 1], preferred_element...  10.2 us
    sub x1, other arithmetic, shards(): total_re = jnp.sum(weight_re * solved_re - weight_im * solved_im, axis=0)  8.35 us
    all_to_all x3, local copies, waits for them, and re-layouts, shards(): lax.all_to_all(grid, 'wave', split_axis=3, concat_axis=0, tiled=True)  6.98 us
  transfers between devices with their start and end apart: 3, of which 3 were waited for; matrix products, arithmetic and copies ran while one was open for 0% of the time, Pallas kernels for 0%

commit v1 on v0

v1 whole, which is shorter than its diff:
```python
import functools

import jax
import jax.numpy as jnp
from jax import lax
from jax.experimental import pallas as pl
from jax.experimental.pallas import tpu as pltpu
from jax.sharding import PartitionSpec as P

F32 = jnp.float32
BF16 = jnp.bfloat16
I32 = jnp.int32
MESH = pl.DeviceIdType.MESH

NY, NZ, NC, NW = 4, 4, 2, 8
NDEG, NLAT = 640, 1280
OWN = 16
HALF = NDEG // NC
QUARTER = HALF // 2
LANES = 128
TILES = NDEG // LANES
MSG = QUARTER + 8
WINDOW = 384
STEPS = 8.0
TOP = 32700.0
BAND = NLAT // NW
ROWS = NY * OWN
CHUNK = 32


def code_of(height):
    return jnp.ceil(jnp.log2(jnp.maximum(height, 1e-30)) * STEPS).astype(I32)


def span_of(code):
    return jnp.exp2(code.astype(F32) * (1.0 / STEPS))


def gain_of(code):
    return TOP * jnp.exp2(code.astype(F32) * (-1.0 / STEPS))


def packed(real, imag, gain):
    high = (real * gain + 32768.5).astype(I32)
    low = (imag * gain + 32768.5).astype(I32)
    return lax.shift_left(high, jnp.full_like(high, 16)) | low


def unpacked(code, step):
    high = lax.shift_right_logical(code, jnp.full_like(code, 16)).astype(F32)
    low = (code & 0xFFFF).astype(F32)
    return (high - 32768.0) * step, (low - 32768.0) * step


def exchange_kernel(
    x_hbm, inv_hbm, w_ref, leg_hbm, out_ref,
    raw_own, raw_pal, w_pal, x_all, leg, snd, rcv, work, rhs_a, rhs_b,
    t_own, t_snd, t_rcv, z_snd, z_rcv, t_fin, grid, pieces,
    raw_own_sem, raw_pal_sem, w_sem, x_snd_sem, x_rcv_sem, x_fwd_sem, leg_sem,
    snd_sem, rcv_sem, t_snd_sem, t_rcv_sem, z_snd_sem, z_rcv_sem, f_snd_sem, f_rcv_sem,
):
    term = lax.axis_index("term")
    wave = lax.axis_index("wave")
    core = lax.rem(term, 2)
    y = lax.rem(term // 2, NY)
    z = term // (2 * NY)
    zy = z * NY + y

    def at(z_, y_, core_, wave_):
        return ((z_ * NY + y_) * 2 + core_, wave_)

    pal = at(z, y, 1 - core, wave)

    def own_copy(j):
        return pltpu.make_async_copy(
            inv_hbm.at[0, :, :, pl.ds(pl.multiple_of(core * HALF, 64), HALF), pl.ds(pl.multiple_of(j * LANES, LANES), LANES)],
            raw_own.at[j],
            raw_own_sem.at[j],
        )

    def pal_copy(j):
        return pltpu.make_async_remote_copy(
            src_ref=inv_hbm.at[0, :, :, pl.ds(pl.multiple_of((1 - core) * HALF, 64), HALF), pl.ds(pl.multiple_of(j * LANES, LANES), LANES)],
            dst_ref=raw_pal.at[j],
            send_sem=raw_pal_sem.at[0, j],
            recv_sem=raw_pal_sem.at[1, j],
            device_id=pal,
            device_id_type=MESH,
        )

    w_copy = pltpu.make_async_remote_copy(
        src_ref=w_ref, dst_ref=w_pal, send_sem=w_sem.at[0], recv_sem=w_sem.at[1], device_id=pal, device_id_type=MESH
    )

    def x_row():
        return pl.ds(pl.multiple_of(zy * OWN, OWN), OWN)

    def x_copy(i):
        peer = lax.rem(zy + i, NZ * NY)
        return pltpu.make_async_remote_copy(
            src_ref=x_hbm.at[lax.rem(peer, NY)],
            dst_ref=x_all.at[core, x_row()],
            send_sem=x_snd_sem.at[i],
            recv_sem=x_rcv_sem.at[i],
            device_id=at(peer // NY, lax.rem(peer, NY), core, wave),
            device_id_type=MESH,
        )

    x_local = pltpu.make_async_copy(x_hbm.at[y], x_all.at[core, x_row()], x_rcv_sem.at[0])
    x_forward = pltpu.make_async_remote_copy(
        src_ref=x_all.at[core],
        dst_ref=x_all.at[core],
        send_sem=x_fwd_sem.at[0],
        recv_sem=x_fwd_sem.at[1],
        device_id=pal,
        device_id_type=MESH,
    )
    leg_copy = pltpu.make_async_copy(leg_hbm.at[y], leg, leg_sem)

    def y_copy(kind, way, j):
        to = lax.rem(y + (1 if way == 0 else NY - 1), NY)
        return pltpu.make_async_remote_copy(
            src_ref=snd.at[kind, way, j],
            dst_ref=rcv.at[kind, way, j],
            send_sem=snd_sem.at[kind, way, j],
            recv_sem=rcv_sem.at[kind, way, j],
            device_id=at(z, to, core, wave),
            device_id_type=MESH,
        )

    def t_copy(j):
        return pltpu.make_async_remote_copy(
            src_ref=t_snd.at[j],
            dst_ref=t_rcv.at[j],
            send_sem=t_snd_sem.at[j],
            recv_sem=t_rcv_sem.at[j],
            device_id=pal,
            device_id_type=MESH,
        )

    def z_copy(i, j):
        return pltpu.make_async_remote_copy(
            src_ref=z_snd.at[i, j],
            dst_ref=z_rcv.at[i, j],
            send_sem=z_snd_sem.at[i, j],
            recv_sem=z_rcv_sem.at[i, j],
            device_id=at(lax.rem(z + 1 + i, NZ), y, core, wave),
            device_id_type=MESH,
        )

    def f_copy(dy, dw):
        to_y = lax.rem(y + dy, NY)
        to_w = lax.rem(wave + dw, NW)
        return pltpu.make_async_remote_copy(
            src_ref=pieces.at[to_y, to_w],
            dst_ref=out_ref.at[y, wave],
            send_sem=f_snd_sem.at[dy, dw],
            recv_sem=f_rcv_sem.at[dy, dw],
            device_id=at(z, to_y, core, to_w),
            device_id_type=MESH,
        )

    def f_arrival(dy, dw):
        from_y = lax.rem(y + NY - dy, NY)
        from_w = lax.rem(wave + NW - dw, NW)
        return pltpu.make_async_remote_copy(
            src_ref=pieces.at[from_y, from_w],
            dst_ref=out_ref.at[from_y, from_w],
            send_sem=f_snd_sem.at[dy, dw],
            recv_sem=f_rcv_sem.at[dy, dw],
            device_id=at(z, from_y, core, from_w),
            device_id_type=MESH,
        )

    def x_arrival(i):
        peer = lax.rem(zy + NZ * NY - i, NZ * NY)
        return pltpu.make_async_remote_copy(
            src_ref=x_hbm.at[y],
            dst_ref=x_all.at[core, pl.ds(pl.multiple_of(peer * OWN, OWN), OWN)],
            send_sem=x_snd_sem.at[i],
            recv_sem=x_rcv_sem.at[i],
            device_id=at(peer // NY, lax.rem(peer, NY), core, wave),
            device_id_type=MESH,
        )

    x_forward_arrival = pltpu.make_async_remote_copy(
        src_ref=x_all.at[1 - core],
        dst_ref=x_all.at[1 - core],
        send_sem=x_fwd_sem.at[0],
        recv_sem=x_fwd_sem.at[1],
        device_id=pal,
        device_id_type=MESH,
    )

    barrier = pltpu.get_barrier_semaphore()
    pl.semaphore_signal(barrier, inc=1, device_id=pal, device_id_type=MESH)

    @pl.loop(1, NZ * NY)
    def _(i):
        peer = lax.rem(zy + i, NZ * NY)
        pl.semaphore_signal(
            barrier, inc=1, device_id=at(peer // NY, lax.rem(peer, NY), core, wave), device_id_type=MESH
        )

    @pl.loop(0, NY * (NW - 1))
    def _(i):
        pl.semaphore_signal(
            barrier,
            inc=1,
            device_id=at(z, i // (NW - 1), core, lax.rem(wave + 1 + lax.rem(i, NW - 1), NW)),
            device_id_type=MESH,
        )

    @pl.loop(0, TILES)
    def _(j):
        own_copy(j).start()

    x_local.start()
    leg_copy.start()
    pad = pl.ds(pl.multiple_of((1 - core) * HALF, 64), WINDOW - HALF)
    for side in range(2):
        rhs_a[side, pad, :] = jnp.zeros((WINDOW - HALF, 2 * LANES), BF16)
        rhs_b[side, pad, :] = jnp.zeros((WINDOW - HALF, 2 * LANES), BF16)
    grid[...] = jnp.zeros_like(grid)

    pl.semaphore_wait(barrier, 1 + (NZ * NY - 1) + NY * (NW - 1))

    w_copy.start()

    @pl.loop(0, TILES)
    def _(j):
        pal_copy(j).start()

    @pl.loop(1, NZ * NY)
    def _(i):
        x_copy(i).start()

    w_copy.wait()
    weights = [w_ref[0:1, 0:1], w_ref[0:1, 1:2], w_pal[0:1, 0:1], w_pal[0:1, 1:2]]
    weights = [jnp.broadcast_to(v, (CHUNK, LANES)) for v in weights]

    def term_sum(j, slot, row):
        rows = pl.ds(row, CHUNK)
        r0 = raw_own[j, slot, 0, rows, :].astype(F32)
        j0 = raw_own[j, slot, 1, rows, :].astype(F32)
        r1 = raw_pal[j, slot, 0, rows, :].astype(F32)
        j1 = raw_pal[j, slot, 1, rows, :].astype(F32)
        a0, b0, a1, b1 = weights
        return (a0 * r0 - b0 * j0) + (a1 * r1 - b1 * j1), (a0 * j0 + b0 * r0) + (a1 * j1 + b1 * r1)

    def higher(height, real, imag):
        tall = jnp.maximum(jnp.abs(real), jnp.abs(imag))
        return jnp.maximum(height, jnp.max(tall.reshape(-1, 8, LANES), axis=0))

    def write_message(to, j, slot, half, since):
        height = jnp.zeros((8, LANES), F32)
        if since is not None:
            step = span_of(since[QUARTER : QUARTER + 8, :])[0:1] * (1.0 / TOP)
            step = jnp.broadcast_to(step, (CHUNK, LANES))
        for part in range(QUARTER // CHUNK):
            rows = slice(part * CHUNK, (part + 1) * CHUNK)
            real, imag = term_sum(j, slot, half * QUARTER + part * CHUNK)
            if since is not None:
                more_real, more_imag = unpacked(since[rows, :], step)
                real, imag = real + more_real, imag + more_imag
            work[0, rows, :] = real
            work[1, rows, :] = imag
            height = higher(height, real, imag)
        height = jnp.broadcast_to(jnp.max(height, axis=0, keepdims=True), (8, LANES))
        code = code_of(height)
        gain = jnp.broadcast_to(gain_of(code)[0:1], (CHUNK, LANES))
        for part in range(QUARTER // CHUNK):
            rows = slice(part * CHUNK, (part + 1) * CHUNK)
            to[rows, :] = packed(work[0, rows, :], work[1, rows, :], gain)
        to[QUARTER : QUARTER + 8, :] = code

    def stage_first(j):
        own_copy(j).wait()
        pal_copy(j).wait_recv()
        for way in range(2):
            write_message(snd.at[0, way, j], j, lax.rem(y + 2, NY), way, None)
            y_copy(0, way, j).start()
        for way in range(2):
            slot = lax.rem(y + (1 if way == 0 else NY - 1), NY)
            write_message(snd.at[1, way, j], j, slot, 1 - way, None)
            y_copy(1, way, j).start()

    def stage_sum(j):
        for way in range(2):
            slot = lax.rem(y + (1 if way == 0 else NY - 1), NY)
            y_copy(0, way, j).wait_recv()
            write_message(snd.at[2, way, j], j, slot, way, rcv.at[0, way, j])
            y_copy(2, way, j).start()

    def stage_product(j):
        for kind in (1, 2):
            for way in range(2):
                y_copy(kind, way, j).wait_recv()
        for half in range(2):
            first = rcv.at[2, half, j]
            second = rcv.at[1, 1 - half, j]
            steps = [
                jnp.broadcast_to(span_of(part[QUARTER : QUARTER + 8, :])[0:1] * (1.0 / TOP), (CHUNK, LANES))
                for part in (first, second)
            ]
            for part in range(QUARTER // CHUNK):
                rows = slice(part * CHUNK, (part + 1) * CHUNK)
                start = half * QUARTER + part * CHUNK
                real, imag = term_sum(j, y, start)
                for source, step in zip((first, second), steps):
                    more_real, more_imag = unpacked(source[rows, :], step)
                    real, imag = real + more_real, imag + more_imag
                real_high = real.astype(BF16)
                imag_high = imag.astype(BF16)
                real_low = (real - real_high.astype(F32)).astype(BF16)
                imag_low = (imag - imag_high.astype(F32)).astype(BF16)
                into = pl.ds(pl.multiple_of(core * (WINDOW - HALF) + start, CHUNK), CHUNK)
                rhs_a[0, into, :] = jnp.concatenate([real_high, imag_high], axis=1)
                rhs_a[1, into, :] = jnp.concatenate([real_low, imag_low], axis=1)
                rhs_b[0, into, :] = jnp.concatenate([-imag_high, real_high], axis=1)
                rhs_b[1, into, :] = jnp.concatenate([-imag_low, real_low], axis=1)

        def product(owner, row):
            rows = pl.ds(pl.multiple_of(row, 128), 128)
            left = x_all[owner, rows, pl.ds(pl.multiple_of(core * 256, LANES), WINDOW)]
            right = x_all[owner, rows, pl.ds(pl.multiple_of(NDEG + core * 256, LANES), WINDOW)]
            value = jnp.dot(left, rhs_a[0], preferred_element_type=F32)
            value += jnp.dot(right, rhs_b[0], preferred_element_type=F32)
            value += jnp.dot(left, rhs_a[1], preferred_element_type=F32)
            value += jnp.dot(right, rhs_b[1], preferred_element_type=F32)
            return value

        @pl.loop(0, 2)
        def _(i):
            t_snd[j, pl.ds(pl.multiple_of(i * 128, 128), 128), :] = product(1 - core, i * 128)

        t_copy(j).start()

        @pl.loop(0, 2)
        def _(i):
            t_own[j, pl.ds(pl.multiple_of(i * 128, 128), 128), :] = product(core, i * 128)

    def stage_spread(j):
        t_copy(j).wait_recv()
        for i in range(NZ):
            to = lax.rem(z + 1 + i, NZ)
            rows = pl.ds(pl.multiple_of(to * ROWS, ROWS), ROWS)
            value = t_own[j, rows, :] + t_rcv[j, rows, :]
            if i == NZ - 1:
                t_fin[j] = value
                continue
            real, imag = value[:, :LANES], value[:, LANES:]
            height = higher(jnp.zeros((8, LANES), F32), real, imag)
            height = jnp.broadcast_to(jnp.max(height, axis=0, keepdims=True), (8, LANES))
            code = code_of(height)
            gain = jnp.broadcast_to(gain_of(code)[0:1], (ROWS, LANES))
            z_snd[i, j, :ROWS, :] = packed(real, imag, gain)
            z_snd[i, j, ROWS:, :] = code
            z_copy(i, j).start()

    def stage_synthesis(j):
        value = t_fin[j]
        real, imag = value[:, :LANES], value[:, LANES:]
        for i in range(NZ - 1):
            z_copy(i, j).wait_recv()
            step = span_of(z_rcv[i, j, ROWS:, :])[0:1] * (1.0 / TOP)
            step = jnp.broadcast_to(step, (ROWS, LANES))
            more_real, more_imag = unpacked(z_rcv[i, j, :ROWS, :], step)
            real, imag = real + more_real, imag + more_imag
        both = jnp.concatenate([real, imag], axis=0)
        high = both.astype(BF16)
        low = (both - high.astype(F32)).astype(BF16)
        left = jnp.concatenate([high, low], axis=0)
        table = pl.ds(pl.multiple_of(j * LANES, LANES), LANES)

        @pl.loop(0, NLAT // 256)
        def _(i):
            columns = pl.ds(pl.multiple_of(i * 256, 256), 256)
            value = jnp.dot(left, leg[table, columns], preferred_element_type=F32)
            grid[:, columns] += value[: 2 * ROWS] + value[2 * ROWS :]

    @pl.loop(0, TILES + 4)
    def _(it):
        @pl.when(it < TILES)
        def _():
            stage_first(it)

        @pl.when((it >= 1) & (it < TILES + 1))
        def _():
            stage_sum(it - 1)

        @pl.when(it == 2)
        def _():
            x_local.wait()

            @pl.loop(1, NZ * NY)
            def _(i):
                x_arrival(i).wait_recv()

            x_forward.start()
            x_forward_arrival.wait_recv()

        @pl.when((it >= 2) & (it < TILES + 2))
        def _():
            stage_product(it - 2)

        @pl.when((it >= 3) & (it < TILES + 3))
        def _():
            stage_spread(it - 3)

        @pl.when(it == 4)
        def _():
            leg_copy.wait()

        @pl.when(it >= 4)
        def _():
            stage_synthesis(it - 4)

    lane = lax.broadcasted_iota(I32, (8, LANES), 1)
    for to_y in range(NY):
        rows = slice(to_y * OWN, (to_y + 1) * OWN)
        real = grid[rows, :]
        imag = grid[ROWS + to_y * OWN : ROWS + (to_y + 1) * OWN, :]
        height = jnp.max(jnp.maximum(jnp.abs(real), jnp.abs(imag)), axis=1, keepdims=True)
        code = code_of(jnp.broadcast_to(height, (OWN, LANES)))
        gain = gain_of(code)
        gain = jnp.concatenate([gain] * (NLAT // LANES), axis=1)
        value = packed(real, imag, gain)
        for to_w in range(NW):
            tile, skip = divmod(to_w * BAND, LANES)
            band = value[:, tile * LANES : tile * LANES + 2 * LANES]
            if skip:
                band = pltpu.roll(band, 2 * LANES - skip, 1)
            rest = band[:, LANES:]
            last = jnp.where(lane < 96, code[:8], code[8:])
            last = jnp.where(lane < 64, pltpu.roll(rest[8:], 32, 1), last)
            last = jnp.where(lane < 32, rest[:8], last)
            pieces[to_y, to_w, :OWN, :] = band[:, :LANES]
            pieces[to_y, to_w, OWN:, :] = last

    @pl.loop(1, NW)
    def _(dw):
        @pl.loop(0, NY)
        def _(dy):
            f_copy(dy, dw).start()

    @pl.loop(1, NY)
    def _(dy):
        f_copy(dy, 0).start()

    out_ref[y, wave] = pieces[y, wave]

    @pl.loop(0, TILES)
    def _(j):
        pal_copy(j).wait_send()
        t_copy(j).wait_send()
        for kind in range(3):
            for way in range(2):
                y_copy(kind, way, j).wait_send()
        for i in range(NZ - 1):
            z_copy(i, j).wait_send()

    @pl.loop(1, NZ * NY)
    def _(i):
        x_copy(i).wait_send()

    x_forward.wait_send()

    @pl.loop(1, NW)
    def _(dw):
        @pl.loop(0, NY)
        def _(dy):
            f_arrival(dy, dw).wait_recv()
            f_copy(dy, dw).wait_send()

    @pl.loop(1, NY)
    def _(dy):
        f_arrival(dy, 0).wait_recv()
        f_copy(dy, 0).wait_send()


def exchange(spectral_state, inverse, term_weights, legendre):
    any_space = pl.BlockSpec(memory_space=pl.ANY)
    vmem = pl.BlockSpec(memory_space=pltpu.VMEM)
    dma = pltpu.SemaphoreType.DMA
    return pl.pallas_call(
        exchange_kernel,
        out_shape=jax.ShapeDtypeStruct((NY, NW, OWN + 8, LANES), I32),
        in_specs=[any_space, any_space, vmem, any_space],
        out_specs=vmem,
        scratch_shapes=[
            pltpu.VMEM((TILES, NY, 2, HALF, LANES), BF16),
            pltpu.VMEM((TILES, NY, 2, HALF, LANES), BF16),
            pltpu.VMEM((1, 2), F32),
            pltpu.VMEM((2, NZ * NY * OWN, 2 * NDEG), BF16),
            pltpu.VMEM((NDEG, NLAT), BF16),
            pltpu.VMEM((3, 2, TILES, MSG, LANES), I32),
            pltpu.VMEM((3, 2, TILES, MSG, LANES), I32),
            pltpu.VMEM((2, QUARTER, LANES), F32),
            pltpu.VMEM((2, WINDOW, 2 * LANES), BF16),
            pltpu.VMEM((2, WINDOW, 2 * LANES), BF16),
            pltpu.VMEM((TILES, 256, 2 * LANES), F32),
            pltpu.VMEM((TILES, 256, 2 * LANES), F32),
            pltpu.VMEM((TILES, 256, 2 * LANES), F32),
            pltpu.VMEM((NZ - 1, TILES, ROWS + 8, LANES), I32),
            pltpu.VMEM((NZ - 1, TILES, ROWS + 8, LANES), I32),
            pltpu.VMEM((TILES, ROWS, 2 * LANES), F32),
            pltpu.VMEM((2 * ROWS, NLAT), F32),
            pltpu.VMEM((NY, NW, OWN + 8, LANES), I32),
            dma((TILES,)),
            dma((2, TILES)),
            dma((2,)),
            dma((NZ * NY,)),
            dma((NZ * NY,)),
            dma((2,)),
            dma,
            dma((3, 2, TILES)),
            dma((3, 2, TILES)),
            dma((TILES,)),
            dma((TILES,)),
            dma((NZ - 1, TILES)),
            dma((NZ - 1, TILES)),
            dma((NY, NW)),
            dma((NY, NW)),
        ],
        compiler_params=pltpu.CompilerParams(
            collective_id=0, has_side_effects=True, vmem_limit_bytes=48 << 20
        ),
        name="exchange",
    )(spectral_state, inverse, term_weights, legendre)


def place_kernel(column_ref, code_ref, out_ref):
    @pl.loop(0, NW)
    def _(from_w):
        for from_y in range(NY):
            column = column_ref[from_w * NY + from_y]
            last = code_ref[from_y, from_w, OWN:, :]
            moved = pltpu.roll(last, LANES - 32, 1)
            for part, rest in ((0, last), (1, moved)):
                step = span_of(rest[:, 64:65]) * (1.0 / TOP)
                main = code_ref[from_y, from_w, part * 8 : part * 8 + 8, :]
                wide = jnp.broadcast_to(step, (8, LANES))
                rows = slice(part * 8, part * 8 + 8)
                for p, value in enumerate(unpacked(main, wide)):
                    out_ref[column, p, rows, :LANES] = value
                for p, value in enumerate(unpacked(rest, wide)):
                    out_ref[column, p, rows, LANES:] = value[:, :32]


def place(slot_column, codes):
    return pl.pallas_call(
        place_kernel,
        out_shape=jax.ShapeDtypeStruct((NW * NY, 2, OWN, BAND), F32),
        in_specs=[pl.BlockSpec(memory_space=pltpu.SMEM), pl.BlockSpec(memory_space=pltpu.VMEM)],
        out_specs=pl.BlockSpec(memory_space=pltpu.VMEM),
        name="place",
    )(slot_column, codes)


def shards(spectral_state, inverse, term_weights, legendre, slot_column):
    codes = exchange(spectral_state, inverse, term_weights, legendre)
    return place(slot_column, codes)


def solution(mesh):
    placed = (
        P("wave", "term", None),
        P("term", "wave", None, None, None),
        P("term", None),
        P("wave", None, None),
        P(),
    )
    return jax.shard_map(
        shards, mesh=mesh, in_specs=placed, out_specs=P(None, None, "term", "wave"), check_vma=False
    )
```

time: 306 us -> 79.1 us (0.26); the launches traced: 302 us -> 79 us
  waiting for transfers between devices: 185 us -> 0 us
  Pallas kernels: 0 us -> 76.7 us
  local copies, waits for them, and re-layouts: 41.4 us -> 2.32 us
  matrix products: 23.5 us -> 0 us
  blocking collectives: 22.9 us -> 0 us
  other arithmetic: 15.7 us -> 0 us
  between operations: 13.2 us -> 0.02 us
    reduce_scatter x2 -> x0, waiting for transfers between devices: 117 us -> none  [the longest x1 94.4 us: summed_rows(): return lax.psum_scatter(pieces, chips, scatter_dimension=0, tiled=True)[0]]
    pallas_call x0 -> x2, Pallas kernels: none -> 76.7 us  [the longest x1 73.5 us: exchange(): pl.pallas_call(exchange_kernel, out_shape=jax.ShapeDtypeStruct((NY, NW, O...]
    all_gather x1 -> x0, waiting for transfers between devices: 66.9 us -> none  [shards(): whole = lax.all_gather(spectral_state, TERM, axis=1, tiled=True)]
    dot_general x4 -> x0, matrix products: 23.5 us -> none  [the longest x1 10.2 us: shards(): jnp.einsum('srn,ksno->ksro', stacked, inverse[:, :, 1], preferred_element...]
    all_to_all x1 -> x0, blocking collectives: 22.9 us -> none  [shards(): lax.all_to_all(grid, 'wave', split_axis=3, concat_axis=0, tiled=True)]
    unnamed x4 -> x6, local copies, waits for them, and re-layouts: 18.1 us -> 2.32 us
    sub x1 -> x0, other arithmetic: 8.35 us -> none  [shards(): total_re = jnp.sum(weight_re * solved_re - weight_im * solved_im, axis=0)]
    all_to_all x3 -> x0, local copies, waits for them, and re-layouts: 6.98 us -> none  [shards(): lax.all_to_all(grid, 'wave', split_axis=3, concat_axis=0, tiled=True)]
  transfers between devices with their start and end apart: 3 -> 0, of which waited for: 3 -> 0; matrix products, arithmetic and copies ran while one was open for 0% -> 0% of each run, Pallas kernels for 0% -> 0%
where the time goes in v1:
time: 79.1 us; the launch traced here: 79 us
  Pallas kernels  76.7 us (97%)
  local copies, waits for them, and re-layouts  2.32 us (3%)
    pallas_call x1, Pallas kernels, exchange(): pl.pallas_call(exchange_kernel, out_shape=jax.ShapeDtypeStruct((NY, NW, O...  73.5 us
    pallas_call x1, Pallas kernels, place(): pl.pallas_call(place_kernel, out_shape=jax.ShapeDtypeStruct((NW * NY, 2,...  3.2 us
    unnamed x6, local copies, waits for them, and re-layouts  2.32 us

profile of v1, /device:TPU:32, one launch (start us, length us, event | category | flops | bytes accessed | tf_op | source)
XLA Modules:
  0.0 79.0 jit_solution(17729186207101731340)
XLA Ops:
  0.0 0.0 copy-start.1
  0.0 0.9 %copy-done.1 = bf16[4,16,1280]{2,1,0:T(8,128)(2,1)S(1)} copy-done((bf16[4,16,1280]{2,1,0:T(8,128)(2,1)S(1)}, bf16[4,16,1280]{2,1,0:T(8,128)(2,1)}, u32[]{:S(2)}) %copy-start.1) | copy-done | bytes 163864
  0.9 0.0 copy-start.2
  0.9 0.7 copy-done.2
  1.6 73.5 %exchange.1.code_ref = s32[4,8,24,128]{3,2,1,0:T(8,128)S(1)} custom-call(bf16[4,16,1280]{2,1,0:T(8,128)(2,1)S(1)} %copy-done.1, bf16[1,4,2,640,640]{4,3,2,1,0:T(8,128)(2,1)} %inv_hbm.1, f32[1,2]{1,0:T(1,128)S(1)} %copy-done.2, bf16[4,640,1280]{2,1,0:T(8,128)(2,1)} %leg_hbm.1), custom_call_target="tpu_custom_call" | custom-call | tf_op jit(solution)/shard_map/exchange/pallas_call | solution.py:486
  75.1 0.0 copy-start
  75.1 0.7 copy-done
  75.8 3.2 %place.1 = f32[32,2,16,160]{3,2,1,0:T(8,128)} custom-call(s32[32]{0:T(128)} %column_ref.1, s32[4,8,24,128]{3,2,1,0:T(8,128)} %copy-done), custom_call_target="tpu_custom_call" | custom-call | tf_op jit(solution)/shard_map/place/pallas_call | solution.py:552
Async XLA Ops:
  0.0 0.9 %copy-start.1 = (bf16[4,16,1280]{2,1,0:T(8,128)(2,1)S(1)}, bf16[4,16,1280]{2,1,0:T(8,128)(2,1)}, u32[]{:S(2)}) copy-start(bf16[4,16,1280]{2,1,0:T(8,128)(2,1)} %x_hbm.1) | copy-start | bytes 491524
  0.9 0.7 copy-start.2
  75.1 0.8 copy-start

commit v2 on v1

--- a/solution.py
+++ b/solution.py
@@ -26,6 +26,7 @@
 BAND = NLAT // NW
 ROWS = NY * OWN
 CHUNK = 32
+MEETINGS = 7
 
 
 def code_of(height):
@@ -53,11 +54,11 @@
 
 
 def exchange_kernel(
-    x_hbm, inv_hbm, w_ref, leg_hbm, out_ref,
-    raw_own, raw_pal, w_pal, x_all, leg, snd, rcv, work, rhs_a, rhs_b,
+    x_hbm, inv_hbm, w_hbm, leg_hbm, out_ref,
+    raw_own, raw_pal, w_ref, w_pal, x_all, leg, snd, rcv, work, rhs_a, rhs_b,
     t_own, t_snd, t_rcv, z_snd, z_rcv, t_fin, grid, pieces,
     raw_own_sem, raw_pal_sem, w_sem, x_snd_sem, x_rcv_sem, x_fwd_sem, leg_sem,
-    snd_sem, rcv_sem, t_snd_sem, t_rcv_sem, z_snd_sem, z_rcv_sem, f_snd_sem, f_rcv_sem,
+    snd_sem, rcv_sem, t_snd_sem, t_rcv_sem, z_snd_sem, z_rcv_sem, f_snd_sem, f_rcv_sem, met,
 ):
     term = lax.axis_index("term")
     wave = lax.axis_index("wave")
@@ -78,35 +79,53 @@
             raw_own_sem.at[j],
         )
 
-    def pal_copy(j):
-        return pltpu.make_async_remote_copy(
-            src_ref=inv_hbm.at[0, :, :, pl.ds(pl.multiple_of((1 - core) * HALF, 64), HALF), pl.ds(pl.multiple_of(j * LANES, LANES), LANES)],
-            dst_ref=raw_pal.at[j],
-            send_sem=raw_pal_sem.at[0, j],
-            recv_sem=raw_pal_sem.at[1, j],
+    def pal_copy(j, d):
+        slot = lax.rem(y + d, NY)
+        return pltpu.make_async_remote_copy(
+            src_ref=inv_hbm.at[0, slot, :, pl.ds(pl.multiple_of((1 - core) * HALF, 64), HALF), pl.ds(pl.multiple_of(j * LANES, LANES), LANES)],
+            dst_ref=raw_pal.at[j, slot],
+            send_sem=raw_pal_sem.at[0, j, d],
+            recv_sem=raw_pal_sem.at[1, j, d],
             device_id=pal,
             device_id_type=MESH,
         )
 
+    w_local = pltpu.make_async_copy(w_hbm, w_ref, w_sem.at[2])
     w_copy = pltpu.make_async_remote_copy(
-        src_ref=w_ref, dst_ref=w_pal, send_sem=w_sem.at[0], recv_sem=w_sem.at[1], device_id=pal, device_id_type=MESH
+        src_ref=w_hbm, dst_ref=w_pal, send_sem=w_sem.at[0], recv_sem=w_sem.at[1], device_id=pal, device_id_type=MESH
     )
 
-    def x_row():
-        return pl.ds(pl.multiple_of(zy * OWN, OWN), OWN)
-
-    def x_copy(i):
-        peer = lax.rem(zy + i, NZ * NY)
-        return pltpu.make_async_remote_copy(
-            src_ref=x_hbm.at[lax.rem(peer, NY)],
-            dst_ref=x_all.at[core, x_row()],
-            send_sem=x_snd_sem.at[i],
-            recv_sem=x_rcv_sem.at[i],
-            device_id=at(peer // NY, lax.rem(peer, NY), core, wave),
-            device_id_type=MESH,
-        )
-
-    x_local = pltpu.make_async_copy(x_hbm.at[y], x_all.at[core, x_row()], x_rcv_sem.at[0])
+    def x_part(z_, y_, size):
+        return x_all.at[core, pl.ds(pl.multiple_of((z_ * NY + y_) * OWN, OWN), size)]
+
+    def x_copy(dy, source):
+        to_y = lax.rem(y + dy, NY)
+        return pltpu.make_async_remote_copy(
+            src_ref=x_hbm.at[to_y],
+            dst_ref=x_part(z, source, OWN),
+            send_sem=x_snd_sem.at[dy],
+            recv_sem=x_rcv_sem.at[dy],
+            device_id=at(z, to_y, core, wave),
+            device_id_type=MESH,
+        )
+
+    def x_arrival(dy):
+        return x_copy(dy, lax.rem(y + NY - dy, NY))
+
+    def x_line_copy(dz, source):
+        return pltpu.make_async_remote_copy(
+            src_ref=x_part(z, 0, ROWS),
+            dst_ref=x_part(source, 0, ROWS),
+            send_sem=x_snd_sem.at[NY + dz],
+            recv_sem=x_rcv_sem.at[NY + dz],
+            device_id=at(lax.rem(z + dz, NZ), y, core, wave),
+            device_id_type=MESH,
+        )
+
+    def x_line_arrival(dz):
+        return x_line_copy(dz, lax.rem(z + NZ - dz, NZ))
+
+    x_local = pltpu.make_async_copy(x_hbm.at[y], x_part(z, y, OWN), x_rcv_sem.at[0])
     x_forward = pltpu.make_async_remote_copy(
         src_ref=x_all.at[core],
         dst_ref=x_all.at[core],
@@ -172,17 +191,6 @@
             device_id_type=MESH,
         )
 
-    def x_arrival(i):
-        peer = lax.rem(zy + NZ * NY - i, NZ * NY)
-        return pltpu.make_async_remote_copy(
-            src_ref=x_hbm.at[y],
-            dst_ref=x_all.at[core, pl.ds(pl.multiple_of(peer * OWN, OWN), OWN)],
-            send_sem=x_snd_sem.at[i],
-            recv_sem=x_rcv_sem.at[i],
-            device_id=at(peer // NY, lax.rem(peer, NY), core, wave),
-            device_id_type=MESH,
-        )
-
     x_forward_arrival = pltpu.make_async_remote_copy(
         src_ref=x_all.at[1 - core],
         dst_ref=x_all.at[1 - core],
@@ -192,29 +200,34 @@
         device_id_type=MESH,
     )
 
+    x_pos = wave // 2
+    high = lax.rem(wave, 2) * NZ + z
+
+    def place_of(x_, y_, high_):
+        return at(lax.rem(high_, NZ), y_, core, x_ * 2 + high_ // NZ)
+
+    around = [
+        place_of(lax.rem(x_pos + 1, 4), y, high),
+        place_of(lax.rem(x_pos + 3, 4), y, high),
+        place_of(x_pos, lax.rem(y + 1, NY), high),
+        place_of(x_pos, lax.rem(y + 3, NY), high),
+        place_of(x_pos, y, lax.rem(high + 1, 2 * NZ)),
+        place_of(x_pos, y, lax.rem(high + 7, 2 * NZ)),
+    ]
+
+    def tell(semaphore):
+        for device in around:
+            pl.semaphore_signal(semaphore, inc=1, device_id=device, device_id_type=MESH)
+
     barrier = pltpu.get_barrier_semaphore()
     pl.semaphore_signal(barrier, inc=1, device_id=pal, device_id_type=MESH)
-
-    @pl.loop(1, NZ * NY)
-    def _(i):
-        peer = lax.rem(zy + i, NZ * NY)
-        pl.semaphore_signal(
-            barrier, inc=1, device_id=at(peer // NY, lax.rem(peer, NY), core, wave), device_id_type=MESH
-        )
-
-    @pl.loop(0, NY * (NW - 1))
-    def _(i):
-        pl.semaphore_signal(
-            barrier,
-            inc=1,
-            device_id=at(z, i // (NW - 1), core, lax.rem(wave + 1 + lax.rem(i, NW - 1), NW)),
-            device_id_type=MESH,
-        )
+    tell(barrier)
 
     @pl.loop(0, TILES)
     def _(j):
         own_copy(j).start()
 
+    w_local.start()
     x_local.start()
     leg_copy.start()
     pad = pl.ds(pl.multiple_of((1 - core) * HALF, 64), WINDOW - HALF)
@@ -223,18 +236,18 @@
         rhs_b[side, pad, :] = jnp.zeros((WINDOW - HALF, 2 * LANES), BF16)
     grid[...] = jnp.zeros_like(grid)
 
-    pl.semaphore_wait(barrier, 1 + (NZ * NY - 1) + NY * (NW - 1))
-
+    pl.semaphore_wait(barrier, 1 + len(around))
     w_copy.start()
 
     @pl.loop(0, TILES)
     def _(j):
-        pal_copy(j).start()
-
-    @pl.loop(1, NZ * NY)
-    def _(i):
-        x_copy(i).start()
-
+        for d in (2, 1, 3, 0):
+            pal_copy(j, d).start()
+
+    tell(met.at[0])
+    x_copy(1, y).start()
+    x_copy(3, y).start()
+    w_local.wait()
     w_copy.wait()
     weights = [w_ref[0:1, 0:1], w_ref[0:1, 1:2], w_pal[0:1, 0:1], w_pal[0:1, 1:2]]
     weights = [jnp.broadcast_to(v, (CHUNK, LANES)) for v in weights]
@@ -276,12 +289,13 @@
 
     def stage_first(j):
         own_copy(j).wait()
-        pal_copy(j).wait_recv()
+        pal_copy(j, 2).wait_recv()
         for way in range(2):
             write_message(snd.at[0, way, j], j, lax.rem(y + 2, NY), way, None)
             y_copy(0, way, j).start()
         for way in range(2):
             slot = lax.rem(y + (1 if way == 0 else NY - 1), NY)
+            pal_copy(j, 1 if way == 0 else NY - 1).wait_recv()
             write_message(snd.at[1, way, j], j, slot, 1 - way, None)
             y_copy(1, way, j).start()
 
@@ -293,6 +307,7 @@
             y_copy(2, way, j).start()
 
     def stage_product(j):
+        pal_copy(j, 0).wait_recv()
         for kind in (1, 2):
             for way in range(2):
                 y_copy(kind, way, j).wait_recv()
@@ -379,7 +394,7 @@
             value = jnp.dot(left, leg[table, columns], preferred_element_type=F32)
             grid[:, columns] += value[: 2 * ROWS] + value[2 * ROWS :]
 
-    @pl.loop(0, TILES + 4)
+    @pl.loop(0, TILES + 5)
     def _(it):
         @pl.when(it < TILES)
         def _():
@@ -389,32 +404,48 @@
         def _():
             stage_sum(it - 1)
 
-        @pl.when(it == 2)
+        @pl.when(it < MEETINGS)
+        def _():
+            pl.semaphore_wait(met.at[it], len(around))
+
+        @pl.when(it < MEETINGS - 1)
+        def _():
+            tell(met.at[it + 1])
+
+        @pl.when(it == 0)
+        def _():
+            x_copy(2, y).start()
+
+        @pl.when(it == 1)
         def _():
             x_local.wait()
-
-            @pl.loop(1, NZ * NY)
-            def _(i):
-                x_arrival(i).wait_recv()
-
+            for dy in range(1, NY):
+                x_arrival(dy).wait_recv()
+            for dz in (2, 1, 3):
+                x_line_copy(dz, z).start()
+
+        @pl.when(it == 3)
+        def _():
+            for dz in (2, 1, 3):
+                x_line_arrival(dz).wait_recv()
             x_forward.start()
             x_forward_arrival.wait_recv()
 
-        @pl.when((it >= 2) & (it < TILES + 2))
-        def _():
-            stage_product(it - 2)
-
         @pl.when((it >= 3) & (it < TILES + 3))
         def _():
-            stage_spread(it - 3)
-
-        @pl.when(it == 4)
+            stage_product(it - 3)
+
+        @pl.when((it >= 4) & (it < TILES + 4))
+        def _():
+            stage_spread(it - 4)
+
+        @pl.when(it == 5)
         def _():
             leg_copy.wait()
 
-        @pl.when(it >= 4)
-        def _():
-            stage_synthesis(it - 4)
+        @pl.when(it >= 5)
+        def _():
+            stage_synthesis(it - 5)
 
     lane = lax.broadcasted_iota(I32, (8, LANES), 1)
     for to_y in range(NY):
@@ -438,21 +469,22 @@
             pieces[to_y, to_w, :OWN, :] = band[:, :LANES]
             pieces[to_y, to_w, OWN:, :] = last
 
-    @pl.loop(1, NW)
-    def _(dw):
-        @pl.loop(0, NY)
-        def _(dy):
+        dy = lax.rem(to_y + NY - y, NY)
+        for dw in (1, 7, 3, 5, 2, 6, 4):
             f_copy(dy, dw).start()
 
-    @pl.loop(1, NY)
-    def _(dy):
-        f_copy(dy, 0).start()
-
-    out_ref[y, wave] = pieces[y, wave]
+        @pl.when(dy != 0)
+        def _():
+            f_copy(dy, 0).start()
+
+
+    stay = pltpu.make_async_copy(pieces.at[y, wave], out_ref.at[y, wave], f_rcv_sem.at[0, 0])
+    stay.start()
 
     @pl.loop(0, TILES)
     def _(j):
-        pal_copy(j).wait_send()
+        for d in range(NY):
+            pal_copy(j, d).wait_send()
         t_copy(j).wait_send()
         for kind in range(3):
             for way in range(2):
@@ -460,11 +492,11 @@
         for i in range(NZ - 1):
             z_copy(i, j).wait_send()
 
-    @pl.loop(1, NZ * NY)
-    def _(i):
-        x_copy(i).wait_send()
-
+    for d in range(1, NY):
+        x_copy(d, y).wait_send()
+        x_line_copy(d, z).wait_send()
     x_forward.wait_send()
+    stay.wait()
 
     @pl.loop(1, NW)
     def _(dw):
@@ -481,16 +513,16 @@
 
 def exchange(spectral_state, inverse, term_weights, legendre):
     any_space = pl.BlockSpec(memory_space=pl.ANY)
-    vmem = pl.BlockSpec(memory_space=pltpu.VMEM)
     dma = pltpu.SemaphoreType.DMA
     return pl.pallas_call(
         exchange_kernel,
         out_shape=jax.ShapeDtypeStruct((NY, NW, OWN + 8, LANES), I32),
-        in_specs=[any_space, any_space, vmem, any_space],
-        out_specs=vmem,
+        in_specs=[any_space] * 4,
+        out_specs=any_space,
         scratch_shapes=[
             pltpu.VMEM((TILES, NY, 2, HALF, LANES), BF16),
             pltpu.VMEM((TILES, NY, 2, HALF, LANES), BF16),
+            pltpu.VMEM((1, 2), F32),
             pltpu.VMEM((1, 2), F32),
             pltpu.VMEM((2, NZ * NY * OWN, 2 * NDEG), BF16),
             pltpu.VMEM((NDEG, NLAT), BF16),
@@ -508,10 +540,10 @@
             pltpu.VMEM((2 * ROWS, NLAT), F32),
             pltpu.VMEM((NY, NW, OWN + 8, LANES), I32),
             dma((TILES,)),
-            dma((2, TILES)),
-            dma((2,)),
-            dma((NZ * NY,)),
-            dma((NZ * NY,)),
+            dma((2, TILES, NY)),
+            dma((3,)),
+            dma((2 * NY,)),
+            dma((2 * NY,)),
             dma((2,)),
             dma,
             dma((3, 2, TILES)),
@@ -522,19 +554,23 @@
             dma((NZ - 1, TILES)),
             dma((NY, NW)),
             dma((NY, NW)),
+            pltpu.SemaphoreType.REGULAR((MEETINGS,)),
         ],
         compiler_params=pltpu.CompilerParams(
-            collective_id=0, has_side_effects=True, vmem_limit_bytes=48 << 20
+            collective_id=0, has_side_effects=True, vmem_limit_bytes=60 * 1024 * 1024
         ),
         name="exchange",
     )(spectral_state, inverse, term_weights, legendre)
 
 
-def place_kernel(column_ref, code_ref, out_ref):
+def place_kernel(column_ref, code_ref, out_hbm, decoded, sem):
+    def out_copy(slot):
+        return pltpu.make_async_copy(decoded.at[slot], out_hbm.at[column_ref[slot]], sem.at[slot])
+
     @pl.loop(0, NW)
     def _(from_w):
         for from_y in range(NY):
-            column = column_ref[from_w * NY + from_y]
+            slot = from_w * NY + from_y
             last = code_ref[from_y, from_w, OWN:, :]
             moved = pltpu.roll(last, LANES - 32, 1)
             for part, rest in ((0, last), (1, moved)):
@@ -543,17 +579,25 @@
                 wide = jnp.broadcast_to(step, (8, LANES))
                 rows = slice(part * 8, part * 8 + 8)
                 for p, value in enumerate(unpacked(main, wide)):
-                    out_ref[column, p, rows, :LANES] = value
+                    decoded[slot, p, rows, :LANES] = value
                 for p, value in enumerate(unpacked(rest, wide)):
-                    out_ref[column, p, rows, LANES:] = value[:, :32]
+                    decoded[slot, p, rows, LANES:] = value[:, :32]
+            out_copy(slot).start()
+
+    @pl.loop(0, NW * NY)
+    def _(slot):
+        out_copy(slot).wait()
 
 
 def place(slot_column, codes):
+    shape = (NW * NY, 2, OWN, BAND)
     return pl.pallas_call(
         place_kernel,
-        out_shape=jax.ShapeDtypeStruct((NW * NY, 2, OWN, BAND), F32),
+        out_shape=jax.ShapeDtypeStruct(shape, F32),
         in_specs=[pl.BlockSpec(memory_space=pltpu.SMEM), pl.BlockSpec(memory_space=pltpu.VMEM)],
-        out_specs=pl.BlockSpec(memory_space=pltpu.VMEM),
+        out_specs=pl.BlockSpec(memory_space=pl.ANY),
+        scratch_shapes=[pltpu.VMEM(shape, F32), pltpu.SemaphoreType.DMA((NW * NY,))],
+        compiler_params=pltpu.CompilerParams(vmem_limit_bytes=60 * 1024 * 1024),
         name="place",
     )(slot_column, codes)
 

time: 79.1 us -> 75.3 us (0.952)
  the two profiles are of different devices: /device:TPU:32 before, /device:TPU:48 now
where the time goes in v2:
time: 75.3 us; the launch traced here: 75.2 us
  Pallas kernels  75.2 us (100%)
    pallas_call x1, Pallas kernels, exchange(): pl.pallas_call(exchange_kernel, out_shape=jax.ShapeDtypeStruct((NY, NW, O...  72 us
    pallas_call x1, Pallas kernels, place(): pl.pallas_call(place_kernel, out_shape=jax.ShapeDtypeStruct(shape, F32),...  3.18 us

profile of v2, /device:TPU:48, one launch (start us, length us, event | category | flops | bytes accessed | tf_op | source)
XLA Modules:
  0.0 75.2 jit_solution(4067466332967723341)
XLA Ops:
  0.0 72.0 %exchange.1.code_ref = s32[4,8,24,128]{3,2,1,0:T(8,128)} custom-call(bf16[4,16,1280]{2,1,0:T(8,128)(2,1)} %x_hbm.1, bf16[1,4,2,640,640]{4,3,2,1,0:T(8,128)(2,1)} %inv_hbm.1, f32[1,2]{1,0:T(1,128)} %w_hbm.1, bf16[4,640,1280]{2,1,0:T(8,128)(2,1)} %leg_hbm.1), custom_call_target="tpu_custom_call" | custom-call | tf_op jit(solution)/shard_map/exchange/pallas_call | solution.py:517
  72.1 3.2 %place.1 = f32[32,2,16,160]{3,2,1,0:T(8,128)} custom-call(s32[32]{0:T(128)} %column_ref.1, s32[4,8,24,128]{3,2,1,0:T(8,128)} %exchange.1.code_ref), custom_call_target="tpu_custom_call" | custom-call | tf_op jit(solution)/shard_map/place/pallas_call | solution.py:594

commit v3 on v2

--- a/solution.py
+++ b/solution.py
@@ -55,7 +55,7 @@
 
 def exchange_kernel(
     x_hbm, inv_hbm, w_hbm, leg_hbm, out_ref,
-    raw_own, raw_pal, w_ref, w_pal, x_all, leg, snd, rcv, work, rhs_a, rhs_b,
+    raw_own, raw_pal, w_ref, w_pal, x_all, leg, snd, rcv, work, rhs,
     t_own, t_snd, t_rcv, z_snd, z_rcv, t_fin, grid, pieces,
     raw_own_sem, raw_pal_sem, w_sem, x_snd_sem, x_rcv_sem, x_fwd_sem, leg_sem,
     snd_sem, rcv_sem, t_snd_sem, t_rcv_sem, z_snd_sem, z_rcv_sem, f_snd_sem, f_rcv_sem, met,
@@ -112,28 +112,58 @@
     def x_arrival(dy):
         return x_copy(dy, lax.rem(y + NY - dy, NY))
 
-    def x_line_copy(dz, source):
-        return pltpu.make_async_remote_copy(
-            src_ref=x_part(z, 0, ROWS),
-            dst_ref=x_part(source, 0, ROWS),
-            send_sem=x_snd_sem.at[NY + dz],
-            recv_sem=x_rcv_sem.at[NY + dz],
-            device_id=at(lax.rem(z + dz, NZ), y, core, wave),
-            device_id_type=MESH,
-        )
-
-    def x_line_arrival(dz):
-        return x_line_copy(dz, lax.rem(z + NZ - dz, NZ))
+    def x_line_copy(way, hop):
+        owner = z + (-hop if way == 0 else hop)
+        to_z = z + (1 if way == 0 else -1)
+        copy = pltpu.make_async_remote_copy(
+            src_ref=x_part(owner, 0, ROWS),
+            dst_ref=x_part(owner, 0, ROWS),
+            send_sem=x_snd_sem.at[NY + 3 * way + hop],
+            recv_sem=x_rcv_sem.at[NY + 3 * way + hop],
+            device_id=at(to_z, y, core, wave),
+            device_id_type=MESH,
+        )
+        inside = (owner >= 0) & (to_z < NZ) if way == 0 else (owner < NZ) & (to_z >= 0)
+        return copy, inside
+
+    def x_line_arrival(way, hop):
+        owner = z + (-1 - hop if way == 0 else 1 + hop)
+        copy = pltpu.make_async_remote_copy(
+            src_ref=x_part(owner, 0, ROWS),
+            dst_ref=x_part(owner, 0, ROWS),
+            send_sem=x_snd_sem.at[NY + 3 * way + hop],
+            recv_sem=x_rcv_sem.at[NY + 3 * way + hop],
+            device_id=pal,
+            device_id_type=MESH,
+        )
+        return copy, owner, (owner >= 0) if way == 0 else (owner < NZ)
+
+    def x_pass(owner, owner_core):
+        part = x_all.at[owner_core, pl.ds(pl.multiple_of(owner * ROWS, ROWS), ROWS)]
+        return pltpu.make_async_remote_copy(
+            src_ref=part,
+            dst_ref=part,
+            send_sem=x_fwd_sem.at[0, owner],
+            recv_sem=x_fwd_sem.at[1, owner],
+            device_id=pal,
+            device_id_type=MESH,
+        )
+
+    def x_line_send(hop):
+        for way in range(2):
+            copy, inside = x_line_copy(way, hop)
+            pl.when(inside)(copy.start)
+
+    def x_line_take(hop):
+        for way in range(2):
+            copy, owner, present = x_line_arrival(way, hop)
+
+            @pl.when(present)
+            def _():
+                copy.wait_recv()
+                x_pass(owner, core).start()
 
     x_local = pltpu.make_async_copy(x_hbm.at[y], x_part(z, y, OWN), x_rcv_sem.at[0])
-    x_forward = pltpu.make_async_remote_copy(
-        src_ref=x_all.at[core],
-        dst_ref=x_all.at[core],
-        send_sem=x_fwd_sem.at[0],
-        recv_sem=x_fwd_sem.at[1],
-        device_id=pal,
-        device_id_type=MESH,
-    )
     leg_copy = pltpu.make_async_copy(leg_hbm.at[y], leg, leg_sem)
 
     def y_copy(kind, way, j):
@@ -167,6 +197,12 @@
             device_id_type=MESH,
         )
 
+    def shifted(z_, steps):
+        return lax.rem(z_ + steps, NZ)
+
+    block = shifted(z, 1 + 2 * core)
+    origin = shifted(z, 3 - 2 * core)
+
     def f_copy(dy, dw):
         to_y = lax.rem(y + dy, NY)
         to_w = lax.rem(wave + dw, NW)
@@ -175,7 +211,7 @@
             dst_ref=out_ref.at[y, wave],
             send_sem=f_snd_sem.at[dy, dw],
             recv_sem=f_rcv_sem.at[dy, dw],
-            device_id=at(z, to_y, core, to_w),
+            device_id=at(block, to_y, core, to_w),
             device_id_type=MESH,
         )
 
@@ -187,18 +223,9 @@
             dst_ref=out_ref.at[from_y, from_w],
             send_sem=f_snd_sem.at[dy, dw],
             recv_sem=f_rcv_sem.at[dy, dw],
-            device_id=at(z, from_y, core, from_w),
-            device_id_type=MESH,
-        )
-
-    x_forward_arrival = pltpu.make_async_remote_copy(
-        src_ref=x_all.at[1 - core],
-        dst_ref=x_all.at[1 - core],
-        send_sem=x_fwd_sem.at[0],
-        recv_sem=x_fwd_sem.at[1],
-        device_id=pal,
-        device_id_type=MESH,
-    )
+            device_id=at(origin, from_y, core, from_w),
+            device_id_type=MESH,
+        )
 
     x_pos = wave // 2
     high = lax.rem(wave, 2) * NZ + z
@@ -230,10 +257,10 @@
     w_local.start()
     x_local.start()
     leg_copy.start()
-    pad = pl.ds(pl.multiple_of((1 - core) * HALF, 64), WINDOW - HALF)
     for side in range(2):
-        rhs_a[side, pad, :] = jnp.zeros((WINDOW - HALF, 2 * LANES), BF16)
-        rhs_b[side, pad, :] = jnp.zeros((WINDOW - HALF, 2 * LANES), BF16)
+        for base in (0, WINDOW):
+            pad = pl.ds(pl.multiple_of(base + (1 - core) * HALF, 64), WINDOW - HALF)
+            rhs[side, pad, :] = jnp.zeros((WINDOW - HALF, 2 * LANES), BF16)
     grid[...] = jnp.zeros_like(grid)
 
     pl.semaphore_wait(barrier, 1 + len(around))
@@ -247,6 +274,9 @@
     tell(met.at[0])
     x_copy(1, y).start()
     x_copy(3, y).start()
+    pl.semaphore_wait(met.at[0], len(around))
+    tell(met.at[1])
+    x_copy(2, y).start()
     w_local.wait()
     w_copy.wait()
     weights = [w_ref[0:1, 0:1], w_ref[0:1, 1:2], w_pal[0:1, 0:1], w_pal[0:1, 1:2]]
@@ -293,6 +323,8 @@
         for way in range(2):
             write_message(snd.at[0, way, j], j, lax.rem(y + 2, NY), way, None)
             y_copy(0, way, j).start()
+
+    def stage_own(j):
         for way in range(2):
             slot = lax.rem(y + (1 if way == 0 else NY - 1), NY)
             pal_copy(j, 1 if way == 0 else NY - 1).wait_recv()
@@ -330,36 +362,28 @@
                 real_low = (real - real_high.astype(F32)).astype(BF16)
                 imag_low = (imag - imag_high.astype(F32)).astype(BF16)
                 into = pl.ds(pl.multiple_of(core * (WINDOW - HALF) + start, CHUNK), CHUNK)
-                rhs_a[0, into, :] = jnp.concatenate([real_high, imag_high], axis=1)
-                rhs_a[1, into, :] = jnp.concatenate([real_low, imag_low], axis=1)
-                rhs_b[0, into, :] = jnp.concatenate([-imag_high, real_high], axis=1)
-                rhs_b[1, into, :] = jnp.concatenate([-imag_low, real_low], axis=1)
-
-        def product(owner, row):
-            rows = pl.ds(pl.multiple_of(row, 128), 128)
-            left = x_all[owner, rows, pl.ds(pl.multiple_of(core * 256, LANES), WINDOW)]
-            right = x_all[owner, rows, pl.ds(pl.multiple_of(NDEG + core * 256, LANES), WINDOW)]
-            value = jnp.dot(left, rhs_a[0], preferred_element_type=F32)
-            value += jnp.dot(right, rhs_b[0], preferred_element_type=F32)
-            value += jnp.dot(left, rhs_a[1], preferred_element_type=F32)
-            value += jnp.dot(right, rhs_b[1], preferred_element_type=F32)
-            return value
-
-        @pl.loop(0, 2)
-        def _(i):
-            t_snd[j, pl.ds(pl.multiple_of(i * 128, 128), 128), :] = product(1 - core, i * 128)
-
+                also = pl.ds(pl.multiple_of(WINDOW + core * (WINDOW - HALF) + start, CHUNK), CHUNK)
+                rhs[0, into, :] = jnp.concatenate([real_high, imag_high], axis=1)
+                rhs[1, into, :] = jnp.concatenate([real_low, imag_low], axis=1)
+                rhs[0, also, :] = jnp.concatenate([-imag_high, real_high], axis=1)
+                rhs[1, also, :] = jnp.concatenate([-imag_low, real_low], axis=1)
+
+        def product(owner):
+            left = x_all[owner, :, pl.ds(pl.multiple_of(core * 256, LANES), WINDOW)]
+            right = x_all[owner, :, pl.ds(pl.multiple_of(NDEG + core * 256, LANES), WINDOW)]
+            both = jnp.concatenate([left, right], axis=1)
+            value = jnp.dot(both, rhs[0], preferred_element_type=F32)
+            return value + jnp.dot(both, rhs[1], preferred_element_type=F32)
+
+        t_snd[j] = product(1 - core)
         t_copy(j).start()
-
-        @pl.loop(0, 2)
-        def _(i):
-            t_own[j, pl.ds(pl.multiple_of(i * 128, 128), 128), :] = product(core, i * 128)
+        t_own[j] = product(core)
 
     def stage_spread(j):
         t_copy(j).wait_recv()
         for i in range(NZ):
             to = lax.rem(z + 1 + i, NZ)
-            rows = pl.ds(pl.multiple_of(to * ROWS, ROWS), ROWS)
+            rows = pl.ds(pl.multiple_of(shifted(to, 1 + 2 * core) * ROWS, ROWS), ROWS)
             value = t_own[j, rows, :] + t_rcv[j, rows, :]
             if i == NZ - 1:
                 t_fin[j] = value
@@ -394,7 +418,7 @@
             value = jnp.dot(left, leg[table, columns], preferred_element_type=F32)
             grid[:, columns] += value[: 2 * ROWS] + value[2 * ROWS :]
 
-    @pl.loop(0, TILES + 5)
+    @pl.loop(0, TILES + 2)
     def _(it):
         @pl.when(it < TILES)
         def _():
@@ -404,54 +428,68 @@
         def _():
             stage_sum(it - 1)
 
-        @pl.when(it < MEETINGS)
-        def _():
-            pl.semaphore_wait(met.at[it], len(around))
+        @pl.when(it < TILES)
+        def _():
+            stage_own(it)
 
         @pl.when(it < MEETINGS - 1)
         def _():
-            tell(met.at[it + 1])
+            pl.semaphore_wait(met.at[it + 1], len(around))
+
+        @pl.when(it < MEETINGS - 2)
+        def _():
+            tell(met.at[it + 2])
 
         @pl.when(it == 0)
-        def _():
-            x_copy(2, y).start()
-
-        @pl.when(it == 1)
         def _():
             x_local.wait()
             for dy in range(1, NY):
                 x_arrival(dy).wait_recv()
-            for dz in (2, 1, 3):
-                x_line_copy(dz, z).start()
+            x_line_send(0)
+            x_pass(z, core).start()
+
+        @pl.when(it == 1)
+        def _():
+            x_line_take(0)
+            x_line_send(1)
+
+        @pl.when(it == 2)
+        def _():
+            x_line_take(1)
+            x_line_send(2)
 
         @pl.when(it == 3)
         def _():
-            for dz in (2, 1, 3):
-                x_line_arrival(dz).wait_recv()
-            x_forward.start()
-            x_forward_arrival.wait_recv()
-
-        @pl.when((it >= 3) & (it < TILES + 3))
-        def _():
-            stage_product(it - 3)
-
-        @pl.when((it >= 4) & (it < TILES + 4))
-        def _():
-            stage_spread(it - 4)
-
-        @pl.when(it == 5)
+            x_line_take(2)
+            for owner in range(NZ):
+                x_pass(owner, 1 - core).wait_recv()
+
+        @pl.when(it >= 3)
+        def _():
+            @pl.loop(jnp.where(it == 3, 0, it - 2), it - 1)
+            def _(j):
+                stage_product(j)
+                stage_spread(j)
+
+        @pl.when(it == 4)
         def _():
             leg_copy.wait()
 
-        @pl.when(it >= 5)
-        def _():
-            stage_synthesis(it - 5)
+        @pl.when(it >= 4)
+        def _():
+            @pl.loop(
+                jnp.where(it == 4, 0, it - 3), jnp.where(it == TILES + 1, TILES, it - 2)
+            )
+            def _(j):
+                stage_synthesis(j)
 
     lane = lax.broadcasted_iota(I32, (8, LANES), 1)
-    for to_y in range(NY):
-        rows = slice(to_y * OWN, (to_y + 1) * OWN)
-        real = grid[rows, :]
-        imag = grid[ROWS + to_y * OWN : ROWS + (to_y + 1) * OWN, :]
+    @pl.loop(0, NY)
+    def _(turn):
+        dy = jnp.where(turn < 3, jnp.where(turn < 1, 2, turn * 2 - 1), 0)
+        to_y = lax.rem(y + dy, NY)
+        real = grid[pl.ds(pl.multiple_of(to_y * OWN, OWN), OWN), :]
+        imag = grid[pl.ds(pl.multiple_of(ROWS + to_y * OWN, OWN), OWN), :]
         height = jnp.max(jnp.maximum(jnp.abs(real), jnp.abs(imag)), axis=1, keepdims=True)
         code = code_of(jnp.broadcast_to(height, (OWN, LANES)))
         gain = gain_of(code)
@@ -469,17 +507,9 @@
             pieces[to_y, to_w, :OWN, :] = band[:, :LANES]
             pieces[to_y, to_w, OWN:, :] = last
 
-        dy = lax.rem(to_y + NY - y, NY)
-        for dw in (1, 7, 3, 5, 2, 6, 4):
+        for dw in (5, 3, 1, 7, 4, 2, 6, 0):
             f_copy(dy, dw).start()
 
-        @pl.when(dy != 0)
-        def _():
-            f_copy(dy, 0).start()
-
-
-    stay = pltpu.make_async_copy(pieces.at[y, wave], out_ref.at[y, wave], f_rcv_sem.at[0, 0])
-    stay.start()
 
     @pl.loop(0, TILES)
     def _(j):
@@ -494,21 +524,19 @@
 
     for d in range(1, NY):
         x_copy(d, y).wait_send()
-        x_line_copy(d, z).wait_send()
-    x_forward.wait_send()
-    stay.wait()
-
-    @pl.loop(1, NW)
+    for hop in range(3):
+        for way in range(2):
+            copy, inside = x_line_copy(way, hop)
+            pl.when(inside)(copy.wait_send)
+    for owner in range(NZ):
+        x_pass(owner, core).wait_send()
+
+    @pl.loop(0, NW)
     def _(dw):
         @pl.loop(0, NY)
         def _(dy):
             f_arrival(dy, dw).wait_recv()
             f_copy(dy, dw).wait_send()
-
-    @pl.loop(1, NY)
-    def _(dy):
-        f_arrival(dy, 0).wait_recv()
-        f_copy(dy, 0).wait_send()
 
 
 def exchange(spectral_state, inverse, term_weights, legendre):
@@ -529,8 +557,7 @@
             pltpu.VMEM((3, 2, TILES, MSG, LANES), I32),
             pltpu.VMEM((3, 2, TILES, MSG, LANES), I32),
             pltpu.VMEM((2, QUARTER, LANES), F32),
-            pltpu.VMEM((2, WINDOW, 2 * LANES), BF16),
-            pltpu.VMEM((2, WINDOW, 2 * LANES), BF16),
+            pltpu.VMEM((2, 2 * WINDOW, 2 * LANES), BF16),
             pltpu.VMEM((TILES, 256, 2 * LANES), F32),
             pltpu.VMEM((TILES, 256, 2 * LANES), F32),
             pltpu.VMEM((TILES, 256, 2 * LANES), F32),
@@ -542,9 +569,9 @@
             dma((TILES,)),
             dma((2, TILES, NY)),
             dma((3,)),
-            dma((2 * NY,)),
-            dma((2 * NY,)),
-            dma((2,)),
+            dma((NY + 6,)),
+            dma((NY + 6,)),
+            dma((2, NZ)),
             dma,
             dma((3, 2, TILES)),
             dma((3, 2, TILES)),

time: 75.3 us -> 70.1 us (0.931)
  the two profiles are of different devices: /device:TPU:48 before, /device:TPU:1 now
where the time goes in v3:
time: 70.1 us; the launch traced here: 70 us
  Pallas kernels  70 us (100%)
    pallas_call x1, Pallas kernels, exchange(): pl.pallas_call(exchange_kernel, out_shape=jax.ShapeDtypeStruct((NY, NW, O...  66.9 us
    pallas_call x1, Pallas kernels, place(): pl.pallas_call(place_kernel, out_shape=jax.ShapeDtypeStruct(shape, F32),...  3.18 us

profile of v3, /device:TPU:1, one launch (start us, length us, event | category | flops | bytes accessed | tf_op | source)
XLA Modules:
  0.0 70.0 jit_solution(9519110237107552811)
XLA Ops:
  0.0 66.9 %exchange.1.code_ref = s32[4,8,24,128]{3,2,1,0:T(8,128)} custom-call(bf16[4,16,1280]{2,1,0:T(8,128)(2,1)} %x_hbm.1, bf16[1,4,2,640,640]{4,3,2,1,0:T(8,128)(2,1)} %inv_hbm.1, f32[1,2]{1,0:T(1,128)} %w_hbm.1, bf16[4,640,1280]{2,1,0:T(8,128)(2,1)} %leg_hbm.1), custom_call_target="tpu_custom_call" | custom-call | tf_op jit(solution)/shard_map/exchange/pallas_call | solution.py:545
  66.9 3.2 %place.1 = f32[32,2,16,160]{3,2,1,0:T(8,128)} custom-call(s32[32]{0:T(128)} %column_ref.1, s32[4,8,24,128]{3,2,1,0:T(8,128)} %exchange.1.code_ref), custom_call_target="tpu_custom_call" | custom-call | tf_op jit(solution)/shard_map/place/pallas_call | solution.py:621

commit v4 on v3

--- a/solution.py
+++ b/solution.py
@@ -19,14 +19,13 @@
 QUARTER = HALF // 2
 LANES = 128
 TILES = NDEG // LANES
-MSG = QUARTER + 8
 WINDOW = 384
 STEPS = 8.0
 TOP = 32700.0
 BAND = NLAT // NW
 ROWS = NY * OWN
 CHUNK = 32
-MEETINGS = 7
+MEETINGS = 6
 
 
 def code_of(height):
@@ -55,9 +54,9 @@
 
 def exchange_kernel(
     x_hbm, inv_hbm, w_hbm, leg_hbm, out_ref,
-    raw_own, raw_pal, w_ref, w_pal, x_all, leg, snd, rcv, work, rhs,
+    raw_own, raw_pal, w_ref, w_pal, x_all, leg, snd, rcv, snd_sum, rcv_sum, work, rhs,
     t_own, t_snd, t_rcv, z_snd, z_rcv, t_fin, grid, pieces,
-    raw_own_sem, raw_pal_sem, w_sem, x_snd_sem, x_rcv_sem, x_fwd_sem, leg_sem,
+    raw_own_sem, raw_snd_sem, raw_pal_sem, w_sem, x_snd_sem, x_rcv_sem, x_fwd_sem, leg_sem,
     snd_sem, rcv_sem, t_snd_sem, t_rcv_sem, z_snd_sem, z_rcv_sem, f_snd_sem, f_rcv_sem, met,
 ):
     term = lax.axis_index("term")
@@ -84,8 +83,8 @@
         return pltpu.make_async_remote_copy(
             src_ref=inv_hbm.at[0, slot, :, pl.ds(pl.multiple_of((1 - core) * HALF, 64), HALF), pl.ds(pl.multiple_of(j * LANES, LANES), LANES)],
             dst_ref=raw_pal.at[j, slot],
-            send_sem=raw_pal_sem.at[0, j, d],
-            recv_sem=raw_pal_sem.at[1, j, d],
+            send_sem=raw_snd_sem,
+            recv_sem=raw_pal_sem.at[j, d],
             device_id=pal,
             device_id_type=MESH,
         )
@@ -169,9 +168,9 @@
     def y_copy(kind, way, j):
         to = lax.rem(y + (1 if way == 0 else NY - 1), NY)
         return pltpu.make_async_remote_copy(
-            src_ref=snd.at[kind, way, j],
-            dst_ref=rcv.at[kind, way, j],
-            send_sem=snd_sem.at[kind, way, j],
+            src_ref=(snd, snd_sum)[kind].at[way, j],
+            dst_ref=(rcv, rcv_sum)[kind].at[way, j],
+            send_sem=snd_sem.at[kind],
             recv_sem=rcv_sem.at[kind, way, j],
             device_id=at(z, to, core, wave),
             device_id_type=MESH,
@@ -181,7 +180,7 @@
         return pltpu.make_async_remote_copy(
             src_ref=t_snd.at[j],
             dst_ref=t_rcv.at[j],
-            send_sem=t_snd_sem.at[j],
+            send_sem=t_snd_sem,
             recv_sem=t_rcv_sem.at[j],
             device_id=pal,
             device_id_type=MESH,
@@ -189,10 +188,10 @@
 
     def z_copy(i, j):
         return pltpu.make_async_remote_copy(
-            src_ref=z_snd.at[i, j],
-            dst_ref=z_rcv.at[i, j],
-            send_sem=z_snd_sem.at[i, j],
-            recv_sem=z_rcv_sem.at[i, j],
+            src_ref=z_snd.at[j, i],
+            dst_ref=z_rcv.at[j, i],
+            send_sem=z_snd_sem,
+            recv_sem=z_rcv_sem.at[j],
             device_id=at(lax.rem(z + 1 + i, NZ), y, core, wave),
             device_id_type=MESH,
         )
@@ -201,7 +200,6 @@
         return lax.rem(z_ + steps, NZ)
 
     block = shifted(z, 1 + 2 * core)
-    origin = shifted(z, 3 - 2 * core)
 
     def f_copy(dy, dw):
         to_y = lax.rem(y + dy, NY)
@@ -209,21 +207,19 @@
         return pltpu.make_async_remote_copy(
             src_ref=pieces.at[to_y, to_w],
             dst_ref=out_ref.at[y, wave],
-            send_sem=f_snd_sem.at[dy, dw],
-            recv_sem=f_rcv_sem.at[dy, dw],
+            send_sem=f_snd_sem,
+            recv_sem=f_rcv_sem,
             device_id=at(block, to_y, core, to_w),
             device_id_type=MESH,
         )
 
-    def f_arrival(dy, dw):
-        from_y = lax.rem(y + NY - dy, NY)
-        from_w = lax.rem(wave + NW - dw, NW)
-        return pltpu.make_async_remote_copy(
-            src_ref=pieces.at[from_y, from_w],
-            dst_ref=out_ref.at[from_y, from_w],
-            send_sem=f_snd_sem.at[dy, dw],
-            recv_sem=f_rcv_sem.at[dy, dw],
-            device_id=at(origin, from_y, core, from_w),
+    def whole(source, target, send_sem, recv_sem):
+        return pltpu.make_async_remote_copy(
+            src_ref=source,
+            dst_ref=target,
+            send_sem=send_sem,
+            recv_sem=recv_sem,
+            device_id=pal,
             device_id_type=MESH,
         )
 
@@ -247,7 +243,8 @@
             pl.semaphore_signal(semaphore, inc=1, device_id=device, device_id_type=MESH)
 
     barrier = pltpu.get_barrier_semaphore()
-    pl.semaphore_signal(barrier, inc=1, device_id=pal, device_id_type=MESH)
+    for device in (pal, at(z, lax.rem(y + 2, NY), core, wave)):
+        pl.semaphore_signal(barrier, inc=1, device_id=device, device_id_type=MESH)
     tell(barrier)
 
     @pl.loop(0, TILES)
@@ -263,7 +260,7 @@
             rhs[side, pad, :] = jnp.zeros((WINDOW - HALF, 2 * LANES), BF16)
     grid[...] = jnp.zeros_like(grid)
 
-    pl.semaphore_wait(barrier, 1 + len(around))
+    pl.semaphore_wait(barrier, 2 + len(around))
     w_copy.start()
 
     @pl.loop(0, TILES)
@@ -271,12 +268,9 @@
         for d in (2, 1, 3, 0):
             pal_copy(j, d).start()
 
+    for dy in (2, 1, 3):
+        x_copy(dy, y).start()
     tell(met.at[0])
-    x_copy(1, y).start()
-    x_copy(3, y).start()
-    pl.semaphore_wait(met.at[0], len(around))
-    tell(met.at[1])
-    x_copy(2, y).start()
     w_local.wait()
     w_copy.wait()
     weights = [w_ref[0:1, 0:1], w_ref[0:1, 1:2], w_pal[0:1, 0:1], w_pal[0:1, 1:2]]
@@ -295,67 +289,62 @@
         tall = jnp.maximum(jnp.abs(real), jnp.abs(imag))
         return jnp.maximum(height, jnp.max(tall.reshape(-1, 8, LANES), axis=0))
 
-    def write_message(to, j, slot, half, since):
+    def step_of(message, rows, size):
+        step = span_of(message[rows : rows + 8, :])[0:1] * (1.0 / TOP)
+        return jnp.broadcast_to(step, (size, LANES))
+
+    def write_message(to, j, slot, halves, since):
         height = jnp.zeros((8, LANES), F32)
-        if since is not None:
-            step = span_of(since[QUARTER : QUARTER + 8, :])[0:1] * (1.0 / TOP)
-            step = jnp.broadcast_to(step, (CHUNK, LANES))
-        for part in range(QUARTER // CHUNK):
-            rows = slice(part * CHUNK, (part + 1) * CHUNK)
-            real, imag = term_sum(j, slot, half * QUARTER + part * CHUNK)
-            if since is not None:
-                more_real, more_imag = unpacked(since[rows, :], step)
-                real, imag = real + more_real, imag + more_imag
-            work[0, rows, :] = real
-            work[1, rows, :] = imag
-            height = higher(height, real, imag)
+        for place, half in enumerate(halves):
+            for part in range(QUARTER // CHUNK):
+                base = part * CHUNK
+                rows = slice(base, base + CHUNK)
+                real, imag = term_sum(j, slot, half * QUARTER + base)
+                if since is not None and place == 0:
+                    more_real, more_imag = unpacked(since[rows, :], step_of(since, QUARTER, CHUNK))
+                    real, imag = real + more_real, imag + more_imag
+                rows = slice(place * QUARTER + base, place * QUARTER + base + CHUNK)
+                work[0, rows, :] = real
+                work[1, rows, :] = imag
+                height = higher(height, real, imag)
         height = jnp.broadcast_to(jnp.max(height, axis=0, keepdims=True), (8, LANES))
         code = code_of(height)
         gain = jnp.broadcast_to(gain_of(code)[0:1], (CHUNK, LANES))
-        for part in range(QUARTER // CHUNK):
+        total = QUARTER * len(halves)
+        for part in range(total // CHUNK):
             rows = slice(part * CHUNK, (part + 1) * CHUNK)
             to[rows, :] = packed(work[0, rows, :], work[1, rows, :], gain)
-        to[QUARTER : QUARTER + 8, :] = code
+        to[total : total + 8, :] = code
 
     def stage_first(j):
         own_copy(j).wait()
         pal_copy(j, 2).wait_recv()
         for way in range(2):
-            write_message(snd.at[0, way, j], j, lax.rem(y + 2, NY), way, None)
+            write_message(snd.at[way, j], j, lax.rem(y + 2, NY), (way,), None)
             y_copy(0, way, j).start()
-
-    def stage_own(j):
-        for way in range(2):
-            slot = lax.rem(y + (1 if way == 0 else NY - 1), NY)
-            pal_copy(j, 1 if way == 0 else NY - 1).wait_recv()
-            write_message(snd.at[1, way, j], j, slot, 1 - way, None)
-            y_copy(1, way, j).start()
 
     def stage_sum(j):
         for way in range(2):
-            slot = lax.rem(y + (1 if way == 0 else NY - 1), NY)
+            d = 1 if way == 0 else NY - 1
+            pal_copy(j, d).wait_recv()
             y_copy(0, way, j).wait_recv()
-            write_message(snd.at[2, way, j], j, slot, way, rcv.at[0, way, j])
-            y_copy(2, way, j).start()
+            write_message(snd_sum.at[way, j], j, lax.rem(y + d, NY), (way, 1 - way), rcv.at[way, j])
+            y_copy(1, way, j).start()
 
     def stage_product(j):
         pal_copy(j, 0).wait_recv()
-        for kind in (1, 2):
-            for way in range(2):
-                y_copy(kind, way, j).wait_recv()
+        for way in range(2):
+            y_copy(1, way, j).wait_recv()
+        steps = [step_of(rcv_sum.at[way, j], HALF, CHUNK) for way in range(2)]
         for half in range(2):
-            first = rcv.at[2, half, j]
-            second = rcv.at[1, 1 - half, j]
-            steps = [
-                jnp.broadcast_to(span_of(part[QUARTER : QUARTER + 8, :])[0:1] * (1.0 / TOP), (CHUNK, LANES))
-                for part in (first, second)
-            ]
             for part in range(QUARTER // CHUNK):
-                rows = slice(part * CHUNK, (part + 1) * CHUNK)
                 start = half * QUARTER + part * CHUNK
                 real, imag = term_sum(j, y, start)
-                for source, step in zip((first, second), steps):
-                    more_real, more_imag = unpacked(source[rows, :], step)
+                for way in range(2):
+                    at_row = part * CHUNK + (0 if way == half else QUARTER)
+                    more_real, more_imag = unpacked(
+                        rcv_sum[way, j, at_row : at_row + CHUNK, :], steps[way]
+                    )
                     real, imag = real + more_real, imag + more_imag
                 real_high = real.astype(BF16)
                 imag_high = imag.astype(BF16)
@@ -393,95 +382,91 @@
             height = jnp.broadcast_to(jnp.max(height, axis=0, keepdims=True), (8, LANES))
             code = code_of(height)
             gain = jnp.broadcast_to(gain_of(code)[0:1], (ROWS, LANES))
-            z_snd[i, j, :ROWS, :] = packed(real, imag, gain)
-            z_snd[i, j, ROWS:, :] = code
+            z_snd[j, i, :ROWS, :] = packed(real, imag, gain)
+            z_snd[j, i, ROWS:, :] = code
             z_copy(i, j).start()
 
     def stage_synthesis(j):
+        whole(z_snd.at[j], z_rcv.at[j], z_snd_sem, z_rcv_sem.at[j]).wait_recv()
         value = t_fin[j]
         real, imag = value[:, :LANES], value[:, LANES:]
         for i in range(NZ - 1):
-            z_copy(i, j).wait_recv()
-            step = span_of(z_rcv[i, j, ROWS:, :])[0:1] * (1.0 / TOP)
+            step = span_of(z_rcv[j, i, ROWS:, :])[0:1] * (1.0 / TOP)
             step = jnp.broadcast_to(step, (ROWS, LANES))
-            more_real, more_imag = unpacked(z_rcv[i, j, :ROWS, :], step)
+            more_real, more_imag = unpacked(z_rcv[j, i, :ROWS, :], step)
             real, imag = real + more_real, imag + more_imag
         both = jnp.concatenate([real, imag], axis=0)
         high = both.astype(BF16)
         low = (both - high.astype(F32)).astype(BF16)
-        left = jnp.concatenate([high, low], axis=0)
+        left = jnp.concatenate([high, low], axis=1)
         table = pl.ds(pl.multiple_of(j * LANES, LANES), LANES)
 
         @pl.loop(0, NLAT // 256)
         def _(i):
             columns = pl.ds(pl.multiple_of(i * 256, 256), 256)
-            value = jnp.dot(left, leg[table, columns], preferred_element_type=F32)
-            grid[:, columns] += value[: 2 * ROWS] + value[2 * ROWS :]
-
-    @pl.loop(0, TILES + 2)
+            part = leg[table, columns]
+            right = jnp.concatenate([part, part], axis=0)
+            grid[:, columns] += jnp.dot(left, right, preferred_element_type=F32)
+
+    @pl.loop(0, 2)
+    def _(j):
+        stage_first(j)
+
+    x_local.wait()
+    for dy in range(1, NY):
+        x_arrival(dy).wait_recv()
+    x_line_send(0)
+    x_pass(z, core).start()
+
+    @pl.loop(0, TILES)
     def _(it):
-        @pl.when(it < TILES)
+        stage_sum(it)
+
+        @pl.when(it < TILES - 2)
         def _():
-            stage_first(it)
-
-        @pl.when((it >= 1) & (it < TILES + 1))
-        def _():
-            stage_sum(it - 1)
-
-        @pl.when(it < TILES)
-        def _():
-            stage_own(it)
-
-        @pl.when(it < MEETINGS - 1)
-        def _():
-            pl.semaphore_wait(met.at[it + 1], len(around))
-
-        @pl.when(it < MEETINGS - 2)
-        def _():
-            tell(met.at[it + 2])
+            stage_first(it + 2)
+
+        pl.semaphore_wait(met.at[it], len(around))
+        tell(met.at[it + 1])
 
         @pl.when(it == 0)
-        def _():
-            x_local.wait()
-            for dy in range(1, NY):
-                x_arrival(dy).wait_recv()
-            x_line_send(0)
-            x_pass(z, core).start()
-
-        @pl.when(it == 1)
         def _():
             x_line_take(0)
             x_line_send(1)
 
-        @pl.when(it == 2)
+        @pl.when(it == 1)
         def _():
             x_line_take(1)
             x_line_send(2)
 
-        @pl.when(it == 3)
+        @pl.when(it == 2)
         def _():
             x_line_take(2)
             for owner in range(NZ):
                 x_pass(owner, 1 - core).wait_recv()
 
-        @pl.when(it >= 3)
+        @pl.when(it > 2)
         def _():
-            @pl.loop(jnp.where(it == 3, 0, it - 2), it - 1)
+            @pl.loop(jnp.where(it == 3, 0, 2), jnp.where(it == 3, 2, 3))
+            def _(j):
+                stage_spread(j)
+
+        @pl.when(it > 1)
+        def _():
+            @pl.loop(jnp.where(it == 2, 0, it - 1), jnp.where(it == 4, TILES, it))
             def _(j):
                 stage_product(j)
-                stage_spread(j)
-
-        @pl.when(it == 4)
-        def _():
-            leg_copy.wait()
-
-        @pl.when(it >= 4)
-        def _():
-            @pl.loop(
-                jnp.where(it == 4, 0, it - 3), jnp.where(it == TILES + 1, TILES, it - 2)
-            )
-            def _(j):
-                stage_synthesis(j)
+
+                @pl.when(it == 4)
+                def _():
+                    stage_spread(j)
+
+    leg_copy.wait()
+    pl.semaphore_wait(met.at[MEETINGS - 1], len(around))
+
+    @pl.loop(0, TILES)
+    def _(j):
+        stage_synthesis(j)
 
     lane = lax.broadcasted_iota(I32, (8, LANES), 1)
     @pl.loop(0, NY)
@@ -511,17 +496,11 @@
             f_copy(dy, dw).start()
 
 
-    @pl.loop(0, TILES)
-    def _(j):
-        for d in range(NY):
-            pal_copy(j, d).wait_send()
-        t_copy(j).wait_send()
-        for kind in range(3):
-            for way in range(2):
-                y_copy(kind, way, j).wait_send()
-        for i in range(NZ - 1):
-            z_copy(i, j).wait_send()
-
+    whole(raw_pal, raw_pal, raw_snd_sem, raw_snd_sem).wait_send()
+    whole(snd, rcv, snd_sem.at[0], snd_sem.at[0]).wait_send()
+    whole(snd_sum, rcv_sum, snd_sem.at[1], snd_sem.at[1]).wait_send()
+    whole(t_snd, t_rcv, t_snd_sem, t_snd_sem).wait_send()
+    whole(z_snd, z_rcv, z_snd_sem, z_snd_sem).wait_send()
     for d in range(1, NY):
         x_copy(d, y).wait_send()
     for hop in range(3):
@@ -531,12 +510,7 @@
     for owner in range(NZ):
         x_pass(owner, core).wait_send()
 
-    @pl.loop(0, NW)
-    def _(dw):
-        @pl.loop(0, NY)
-        def _(dy):
-            f_arrival(dy, dw).wait_recv()
-            f_copy(dy, dw).wait_send()
+    whole(pieces, out_ref, f_snd_sem, f_rcv_sem).wait()
 
 
 def exchange(spectral_state, inverse, term_weights, legendre):
@@ -554,33 +528,36 @@
             pltpu.VMEM((1, 2), F32),
             pltpu.VMEM((2, NZ * NY * OWN, 2 * NDEG), BF16),
             pltpu.VMEM((NDEG, NLAT), BF16),
-            pltpu.VMEM((3, 2, TILES, MSG, LANES), I32),
-            pltpu.VMEM((3, 2, TILES, MSG, LANES), I32),
-            pltpu.VMEM((2, QUARTER, LANES), F32),
+            pltpu.VMEM((2, TILES, QUARTER + 8, LANES), I32),
+            pltpu.VMEM((2, TILES, QUARTER + 8, LANES), I32),
+            pltpu.VMEM((2, TILES, HALF + 8, LANES), I32),
+            pltpu.VMEM((2, TILES, HALF + 8, LANES), I32),
+            pltpu.VMEM((2, HALF, LANES), F32),
             pltpu.VMEM((2, 2 * WINDOW, 2 * LANES), BF16),
             pltpu.VMEM((TILES, 256, 2 * LANES), F32),
             pltpu.VMEM((TILES, 256, 2 * LANES), F32),
             pltpu.VMEM((TILES, 256, 2 * LANES), F32),
-            pltpu.VMEM((NZ - 1, TILES, ROWS + 8, LANES), I32),
-            pltpu.VMEM((NZ - 1, TILES, ROWS + 8, LANES), I32),
+            pltpu.VMEM((TILES, NZ - 1, ROWS + 8, LANES), I32),
+            pltpu.VMEM((TILES, NZ - 1, ROWS + 8, LANES), I32),
             pltpu.VMEM((TILES, ROWS, 2 * LANES), F32),
             pltpu.VMEM((2 * ROWS, NLAT), F32),
             pltpu.VMEM((NY, NW, OWN + 8, LANES), I32),
             dma((TILES,)),
-            dma((2, TILES, NY)),
+            dma,
+            dma((TILES, NY)),
             dma((3,)),
             dma((NY + 6,)),
             dma((NY + 6,)),
             dma((2, NZ)),
             dma,
-            dma((3, 2, TILES)),
-            dma((3, 2, TILES)),
+            dma((2,)),
+            dma((2, 2, TILES)),
+            dma,
             dma((TILES,)),
+            dma,
             dma((TILES,)),
-            dma((NZ - 1, TILES)),
-            dma((NZ - 1, TILES)),
-            dma((NY, NW)),
-            dma((NY, NW)),
+            dma,
+            dma,
             pltpu.SemaphoreType.REGULAR((MEETINGS,)),
         ],
         compiler_params=pltpu.CompilerParams(
@@ -594,9 +571,11 @@
     def out_copy(slot):
         return pltpu.make_async_copy(decoded.at[slot], out_hbm.at[column_ref[slot]], sem.at[slot])
 
-    @pl.loop(0, NW)
-    def _(from_w):
-        for from_y in range(NY):
+    @pl.loop(0, NW // 4)
+    def _(group):
+        for index in range(4 * NY):
+            from_w = group * 4 + index // NY
+            from_y = index % NY
             slot = from_w * NY + from_y
             last = code_ref[from_y, from_w, OWN:, :]
             moved = pltpu.roll(last, LANES - 32, 1)

time: 70.1 us -> 64.3 us (0.917)
  the two profiles are of different devices: /device:TPU:1 before, /device:TPU:32 now
where the time goes in v4:
time: 64.3 us; the launch traced here: 63.3 us
  Pallas kernels  63.2 us (98%)
    pallas_call x1, Pallas kernels, exchange(): pl.pallas_call(exchange_kernel, out_shape=jax.ShapeDtypeStruct((NY, NW, O...  60.8 us
    pallas_call x1, Pallas kernels, place(): pl.pallas_call(place_kernel, out_shape=jax.ShapeDtypeStruct(shape, F32),...  2.4 us

profile of v4, /device:TPU:32, one launch (start us, length us, event | category | flops | bytes accessed | tf_op | source)
XLA Modules:
  0.0 63.3 jit_solution(234921771089472574)
XLA Ops:
  0.0 60.8 %exchange.1.code_ref = s32[4,8,24,128]{3,2,1,0:T(8,128)} custom-call(bf16[4,16,1280]{2,1,0:T(8,128)(2,1)} %x_hbm.1, bf16[1,4,2,640,640]{4,3,2,1,0:T(8,128)(2,1)} %inv_hbm.1, f32[1,2]{1,0:T(1,128)} %w_hbm.1, bf16[4,640,1280]{2,1,0:T(8,128)(2,1)} %leg_hbm.1), custom_call_target="tpu_custom_call" | custom-call | tf_op jit(solution)/shard_map/exchange/pallas_call | solution.py:519
  60.9 2.4 %place.1 = f32[32,2,16,160]{3,2,1,0:T(8,128)} custom-call(s32[32]{0:T(128)} %column_ref.1, s32[4,8,24,128]{3,2,1,0:T(8,128)} %exchange.1.code_ref), custom_call_target="tpu_custom_call" | custom-call | tf_op jit(solution)/shard_map/place/pallas_call | solution.py:600

commit v5 on v4

--- a/solution.py
+++ b/solution.py
@@ -199,7 +199,7 @@
     def shifted(z_, steps):
         return lax.rem(z_ + steps, NZ)
 
-    block = shifted(z, 1 + 2 * core)
+    block = shifted(z, NZ // 2)
 
     def f_copy(dy, dw):
         to_y = lax.rem(y + dy, NY)
@@ -333,13 +333,17 @@
 
     def stage_product(j):
         pal_copy(j, 0).wait_recv()
+        for part in range(HALF // CHUNK):
+            rows = slice(part * CHUNK, (part + 1) * CHUNK)
+            work[0, rows, :], work[1, rows, :] = term_sum(j, y, part * CHUNK)
         for way in range(2):
             y_copy(1, way, j).wait_recv()
         steps = [step_of(rcv_sum.at[way, j], HALF, CHUNK) for way in range(2)]
         for half in range(2):
             for part in range(QUARTER // CHUNK):
                 start = half * QUARTER + part * CHUNK
-                real, imag = term_sum(j, y, start)
+                real = work[0, start : start + CHUNK, :]
+                imag = work[1, start : start + CHUNK, :]
                 for way in range(2):
                     at_row = part * CHUNK + (0 if way == half else QUARTER)
                     more_real, more_imag = unpacked(
@@ -370,13 +374,12 @@
 
     def stage_spread(j):
         t_copy(j).wait_recv()
-        for i in range(NZ):
-            to = lax.rem(z + 1 + i, NZ)
-            rows = pl.ds(pl.multiple_of(shifted(to, 1 + 2 * core) * ROWS, ROWS), ROWS)
+        own_rows = pl.ds(pl.multiple_of(block * ROWS, ROWS), ROWS)
+        for turn in range(NZ - 1):
+            middle = (1, 0, 2)[turn]
+            i = jnp.where(z == 0, NZ - 2 - turn, jnp.where(z == NZ - 1, turn, middle))
+            rows = pl.ds(pl.multiple_of(shifted(z + 1 + i, NZ // 2) * ROWS, ROWS), ROWS)
             value = t_own[j, rows, :] + t_rcv[j, rows, :]
-            if i == NZ - 1:
-                t_fin[j] = value
-                continue
             real, imag = value[:, :LANES], value[:, LANES:]
             height = higher(jnp.zeros((8, LANES), F32), real, imag)
             height = jnp.broadcast_to(jnp.max(height, axis=0, keepdims=True), (8, LANES))
@@ -385,6 +388,7 @@
             z_snd[j, i, :ROWS, :] = packed(real, imag, gain)
             z_snd[j, i, ROWS:, :] = code
             z_copy(i, j).start()
+        t_fin[j] = t_own[j, own_rows, :] + t_rcv[j, own_rows, :]
 
     def stage_synthesis(j):
         whole(z_snd.at[j], z_rcv.at[j], z_snd_sem, z_rcv_sem.at[j]).wait_recv()

time: 64.3 us -> 63.1 us (0.981); the launches traced: 63.3 us -> 63 us
  no operation moved by 1% of the time
where the time goes in v5:
time: 63.1 us; the launch traced here: 63 us
  Pallas kernels  63 us (100%)
    pallas_call x1, Pallas kernels, exchange(): pl.pallas_call(exchange_kernel, out_shape=jax.ShapeDtypeStruct((NY, NW, O...  60.6 us
    pallas_call x1, Pallas kernels, place(): pl.pallas_call(place_kernel, out_shape=jax.ShapeDtypeStruct(shape, F32),...  2.4 us

profile of v5, /device:TPU:32, one launch (start us, length us, event | category | flops | bytes accessed | tf_op | source)
XLA Modules:
  0.0 63.0 jit_solution(3634942268608382506)
XLA Ops:
  0.0 60.6 %exchange.1.code_ref = s32[4,8,24,128]{3,2,1,0:T(8,128)} custom-call(bf16[4,16,1280]{2,1,0:T(8,128)(2,1)} %x_hbm.1, bf16[1,4,2,640,640]{4,3,2,1,0:T(8,128)(2,1)} %inv_hbm.1, f32[1,2]{1,0:T(1,128)} %w_hbm.1, bf16[4,640,1280]{2,1,0:T(8,128)(2,1)} %leg_hbm.1), custom_call_target="tpu_custom_call" | custom-call | tf_op jit(solution)/shard_map/exchange/pallas_call | solution.py:523
  60.6 2.4 %place.1 = f32[32,2,16,160]{3,2,1,0:T(8,128)} custom-call(s32[32]{0:T(128)} %column_ref.1, s32[4,8,24,128]{3,2,1,0:T(8,128)} %exchange.1.code_ref), custom_call_target="tpu_custom_call" | custom-call | tf_op jit(solution)/shard_map/place/pallas_call | solution.py:604

commit v6 on v5

--- a/solution.py
+++ b/solution.py
@@ -254,12 +254,6 @@
     w_local.start()
     x_local.start()
     leg_copy.start()
-    for side in range(2):
-        for base in (0, WINDOW):
-            pad = pl.ds(pl.multiple_of(base + (1 - core) * HALF, 64), WINDOW - HALF)
-            rhs[side, pad, :] = jnp.zeros((WINDOW - HALF, 2 * LANES), BF16)
-    grid[...] = jnp.zeros_like(grid)
-
     pl.semaphore_wait(barrier, 2 + len(around))
     w_copy.start()
 
@@ -422,6 +416,12 @@
     x_line_send(0)
     x_pass(z, core).start()
 
+    for side in range(2):
+        for base in (0, WINDOW):
+            pad = pl.ds(pl.multiple_of(base + (1 - core) * HALF, 64), WINDOW - HALF)
+            rhs[side, pad, :] = jnp.zeros((WINDOW - HALF, 2 * LANES), BF16)
+    grid[...] = jnp.zeros_like(grid)
+
     @pl.loop(0, TILES)
     def _(it):
         stage_sum(it)
@@ -496,7 +496,7 @@
             pieces[to_y, to_w, :OWN, :] = band[:, :LANES]
             pieces[to_y, to_w, OWN:, :] = last
 
-        for dw in (5, 3, 1, 7, 4, 2, 6, 0):
+        for dw in (4, 5, 3, 2, 6, 1, 7, 0):
             f_copy(dy, dw).start()
 
 

time: 63.1 us -> 63.1 us (level)
  no operation moved by 1% of the time
where the time goes in v6:
time: 63.1 us; the launch traced here: 63 us
  Pallas kernels  63 us (100%)
    pallas_call x1, Pallas kernels, exchange(): pl.pallas_call(exchange_kernel, out_shape=jax.ShapeDtypeStruct((NY, NW, O...  60.6 us
    pallas_call x1, Pallas kernels, place(): pl.pallas_call(place_kernel, out_shape=jax.ShapeDtypeStruct(shape, F32),...  2.4 us

profile of v6, /device:TPU:32, one launch (start us, length us, event | category | flops | bytes accessed | tf_op | source)
XLA Modules:
  0.0 63.0 jit_solution(10679186632855747756)
XLA Ops:
  0.0 60.6 %exchange.1.code_ref = s32[4,8,24,128]{3,2,1,0:T(8,128)} custom-call(bf16[4,16,1280]{2,1,0:T(8,128)(2,1)} %x_hbm.1, bf16[1,4,2,640,640]{4,3,2,1,0:T(8,128)(2,1)} %inv_hbm.1, f32[1,2]{1,0:T(1,128)} %w_hbm.1, bf16[4,640,1280]{2,1,0:T(8,128)(2,1)} %leg_hbm.1), custom_call_target="tpu_custom_call" | custom-call | tf_op jit(solution)/shard_map/exchange/pallas_call | solution.py:523
  60.6 2.4 %place.1 = f32[32,2,16,160]{3,2,1,0:T(8,128)} custom-call(s32[32]{0:T(128)} %column_ref.1, s32[4,8,24,128]{3,2,1,0:T(8,128)} %exchange.1.code_ref), custom_call_target="tpu_custom_call" | custom-call | tf_op jit(solution)/shard_map/place/pallas_call | solution.py:604
